TPU v7x, 128 devices: a whole 4x4x4 slice. The times are simulated.
128 devices in a mesh: ctx: 16 (over z_hi, x, core), head: 8 (over z_lo, y).
Axes of the slice: x: 4, y: 4, z: 4 (z_hi: 2, z_lo: 2; z = z_hi * 2 + z_lo), core: 2. Of those that a mesh axis runs over, the one named last changes fastest.
Arguments:
- query: bfloat16 [4096, 64, 192], P('ctx', 'head'), may hold values from -12 to 12
- latents: bfloat16 [4096, 576], P('ctx'), may hold values from -4 to 4
- lat_scale: float32 [4096], P('ctx'), may hold values from 0.5 to 2
- doc_lengths: int32 [8], replicated, may hold values from 1 to 3072, 4096 in all
- w_uk: bfloat16 [64, 128, 512], P('head'), may hold values from -0.5 to 0.5
- w_uv: bfloat16 [64, 512, 128], P('head'), may hold values from -0.25 to 0.25
- w_o: bfloat16 [8192, 7168], P('head'), may hold values from -0.09375 to 0.09375
Outputs:
- attn_out: bfloat16 [4096, 7168], P('ctx', 'head')
Inputs may be any that keep to these rules, and one draw needn't show every extreme that they name: `doc_lengths`: 8 lengths that sum to 4096; the longest is exactly 3072.
All inputs are finite; a program needn't handle non-finite values.
Results may differ from a plain program's by a relative error of at most 0.03.
Values may be sent and summed in bfloat16 or wider, within the bound.
A program may use at most 128 MiB of HBM per device.

v0:
```python
import jax
import jax.numpy as jnp
from jax import lax
from jax.sharding import PartitionSpec as P

LAT = 512
NOPE = 128
QDIM = 192
VDIM = 128


def segment_ids(positions, doc_ends):
    return jnp.sum((positions[:, None] >= doc_ends[None, :]).astype(jnp.int32), axis=1)


def attend(carried, query_block, query_pos, query_seg, values, key_pos, key_seg, score_scale):
    running_max, denominator, weighted = carried
    scores = (
        jnp.einsum("qhc,kc->qhk", query_block, values, preferred_element_type=jnp.float32)
        * score_scale
    )
    allowed = (key_pos[None, :] <= query_pos[:, None]) & (key_seg[None, :] == query_seg[:, None])
    scores = jnp.where(allowed[:, None, :], scores, -1e30)
    new_max = jnp.maximum(running_max, jnp.max(scores, axis=2))
    weights = jnp.where(allowed[:, None, :], jnp.exp(scores - new_max[:, :, None]), 0.0)
    rescale = jnp.exp(running_max - new_max)
    denominator = denominator * rescale + jnp.sum(weights, axis=2)
    weighted = weighted * rescale[:, :, None] + jnp.einsum(
        "qhk,kl->qhl",
        weights.astype(jnp.bfloat16),
        values[:, :LAT],
        preferred_element_type=jnp.float32,
    )
    return (new_max, denominator, weighted)


def dequantize(latent_rows, scale_rows):
    scaled = (latent_rows[:, :LAT].astype(jnp.float32) * scale_rows[:, None]).astype(jnp.bfloat16)
    return jnp.concatenate([scaled, latent_rows[:, LAT:]], axis=1)


def tile_length():
    return 256


def shards(query, latents, lat_scale, doc_lengths, w_uk, w_uv, w_o):
    tok_rows = query.shape[0]
    head_count = query.shape[1]
    half_rows = tok_rows // 2
    ctx_index = lax.axis_index("ctx")
    score_scale = float(QDIM) ** (-0.5)
    second_first = ctx_index * tok_rows + half_rows
    doc_ends = jnp.cumsum(doc_lengths)
    offsets = jnp.arange(half_rows, dtype=jnp.int32)
    pos_first = ctx_index * tok_rows + offsets
    pos_second = second_first + offsets
    query_latent = jnp.einsum(
        "thn,hnl->thl", query[:, :, :NOPE], w_uk, preferred_element_type=jnp.float32
    ).astype(jnp.bfloat16)
    query_full = jnp.concatenate([query_latent, query[:, :, NOPE:]], axis=2)
    halves = (
        (query_full[:half_rows], pos_first, segment_ids(pos_first, doc_ends)),
        (query_full[half_rows:], pos_second, segment_ids(pos_second, doc_ends)),
    )
    one_half = (
        jnp.full((half_rows, head_count), -1e30, jnp.float32),
        jnp.zeros((half_rows, head_count), jnp.float32),
        jnp.zeros((half_rows, head_count, LAT), jnp.float32),
    )
    initial = (one_half, one_half)
    latent_rows = lax.all_gather(latents, "ctx", axis=0, tiled=True)
    scale_rows = lax.all_gather(lat_scale.astype(jnp.bfloat16), "ctx", axis=0, tiled=True).astype(
        jnp.float32
    )
    tile_rows = tile_length()
    tile_count = latent_rows.shape[0] // tile_rows

    def tile_step(tile_index, carried_state):
        tile_latent = lax.dynamic_slice_in_dim(latent_rows, tile_index * tile_rows, tile_rows, 0)
        tile_scale = lax.dynamic_slice_in_dim(scale_rows, tile_index * tile_rows, tile_rows, 0)
        values = dequantize(tile_latent, tile_scale)
        key_pos = tile_index * tile_rows + jnp.arange(tile_rows, dtype=jnp.int32)
        key_seg = segment_ids(key_pos, doc_ends)
        updated = []
        for (query_block, query_pos, query_seg), half_state in zip(halves, carried_state):
            needed = (key_pos[0] <= query_pos[-1]) & (key_seg[-1] >= query_seg[0])

            def update(
                inner_state, query_block=query_block, query_pos=query_pos, query_seg=query_seg
            ):
                return attend(
                    inner_state,
                    query_block,
                    query_pos,
                    query_seg,
                    values,
                    key_pos,
                    key_seg,
                    score_scale,
                )

            def unchanged(inner_state):
                return inner_state

            updated.append(lax.cond(needed, update, unchanged, half_state))
        return tuple(updated)

    final_state = lax.fori_loop(0, tile_count, tile_step, initial)
    context = jnp.concatenate(
        [
            (weighted / denominator[:, :, None]).astype(jnp.bfloat16)
            for running_max, denominator, weighted in final_state
        ],
        axis=0,
    )
    head_out = jnp.einsum("thl,hlv->thv", context, w_uv, preferred_element_type=jnp.float32)
    head_out = head_out.astype(jnp.bfloat16).reshape(tok_rows, head_count * VDIM)
    partial_value = jnp.dot(head_out, w_o, preferred_element_type=jnp.float32)
    return lax.psum_scatter(
        partial_value.astype(jnp.bfloat16), "head", scatter_dimension=1, tiled=True
    )


def solution(mesh):
    placed = (
        P("ctx", "head", None),
        P("ctx", None),
        P("ctx"),
        P(),
        P("head", None, None),
        P("head", None, None),
        P("head", None),
    )
    return jax.shard_map(
        shards, mesh=mesh, in_specs=placed, out_specs=P("ctx", "head"), check_vma=False
    )
```

profile of v0, /device:TPU:70, one launch (start us, length us, event | category | flops | bytes accessed | tf_op | source)
XLA Modules:
  0.0 405.9 jit_solution(3430833573118335015)
XLA Ops:
  6.5 1.9 copy.22
  9.3 0.8 reduce-window.8
  10.1 18.4 %all-gather = bf16[16,1,256]{2,1,0:T(2,128)(2,1)S(1)} all-gather(bf16[1,1,256]{2,1,0:T(2,128)(2,1)S(1)} %reshape.155), channel_id=1, replica_groups=mesh['ctx'=16,'head'=8] {'ctx'}, dimensions={0}, use_global_device_ids=true | all-gather | bytes 8704 | tf_op jit(solution)/shard_map/all_gather | solution.py:72
  28.6 1.8 convert_bitcast_fusion
  30.4 2.1 pad_maximum_fusion.1
  32.5 35.8 %all-gather.3.cloned.1.call-done = bf16[4096,576]{1,0:T(8,128)(2,1)} async-done(((bf16[256,576]{1,0:T(8,128)(2,1)}), bf16[4096,576]{1,0:T(8,128)(2,1)}) %all-gather.3.cloned.1.call-update) | async-done | bytes 4718608 | tf_op jit(solution)/shard_map/all_gather | solution.py:71
  68.6 1.6 broadcast_in_dim.74
  70.2 158.0 %while.23 = (s32[]{:T(128)}, f32[128,8]{0,1:T(8,128)S(1)}, f32[128,8]{0,1:T(8,128)S(1)}, f32[128,8,512]{2,0,1:T(8,128)}, f32[128,8]{0,1:T(8,128)S(1)}, /*index=5...) while((s32[]{:T(128)}, f32[128,8]{0,1:T(8,128)S(1)}, ...), condition=%wide.region_13.14_spmd, body=%wide.region_3.13_spmd.sunk | while | flops 1148856320 | bytes 36516544 | solution.py:108
  76.5 0.8 dynamic-slice.6
  77.4 1.1 multiply_convert_fusion.2
  78.5 0.8 pad_maximum_fusion.3
  85.6 0.8 dynamic-slice.6
  86.4 1.1 multiply_convert_fusion.2
  87.5 0.8 pad_maximum_fusion.3
  94.6 0.8 dynamic-slice.6
  95.4 1.1 multiply_convert_fusion.2
  96.5 0.8 pad_maximum_fusion.3
  103.6 0.8 dynamic-slice.6
  104.4 1.1 multiply_convert_fusion.2
  105.5 0.8 pad_maximum_fusion.3
  112.6 0.8 dynamic-slice.6
  113.4 1.1 multiply_convert_fusion.2
  114.5 0.8 pad_maximum_fusion.3
  121.6 0.8 dynamic-slice.6
  122.4 1.1 multiply_convert_fusion.2
  123.5 0.8 pad_maximum_fusion.3
  130.6 0.8 dynamic-slice.6
  131.4 1.1 multiply_convert_fusion.2
  132.5 0.8 pad_maximum_fusion.3
  139.6 0.8 dynamic-slice.6
  140.4 1.1 multiply_convert_fusion.2
  148.6 0.8 dynamic-slice.6
  149.5 1.1 multiply_convert_fusion.2
  157.6 0.8 dynamic-slice.6
  158.5 1.1 multiply_convert_fusion.2
  166.6 0.8 dynamic-slice.6
  167.5 1.1 multiply_convert_fusion.2
  175.6 0.8 dynamic-slice.6
  176.5 1.1 multiply_convert_fusion.2
  184.6 0.8 dynamic-slice.6
  185.5 1.1 multiply_convert_fusion.2
  193.6 0.8 dynamic-slice.6
  194.5 1.1 multiply_convert_fusion.2
  196.3 5.1 %conditional.4 = ((f32[128,8]{0,1:T(8,128)S(1)}, f32[128,8]{0,1:T(8,128)S(1)}, f32[128,8,512]{2,0,1:T(8,128)})) conditional(s32[]{:T(128)} %bitcast.41, (f32[128,8]{0,1:T(8,128)S(1)}, f32[128,8]{0,1:T(8,128)S(1)}, f32[128,8,512]{2,0,1:T(8,128)}) %tuple.59, (s32[256]{0:T(256)S(1)}, s32[128]{0:T(128)S(1)}, s32[256]{0:T(256)S(1)}, s32[128]{0:T(128)S(1)}, ...), branch_computations={%region_5.5_spmd, %region_6.8_spmd} | conditional | flops 573933568 | bytes 26053720 | solution.py:105
  196.4 2.2 fusion.30
  199.1 1.0 multiply_add_fusion
  200.1 1.4 copy-done.2
  207.8 0.8 dynamic-slice.6
  208.6 1.1 multiply_convert_fusion.2
  210.4 5.1 %conditional.4 = ((f32[128,8]{0,1:T(8,128)S(1)}, f32[128,8]{0,1:T(8,128)S(1)}, f32[128,8,512]{2,0,1:T(8,128)})) conditional(s32[]{:T(128)} %bitcast.41, (f32[128,8]{0,1:T(8,128)S(1)}, f32[128,8]{0,1:T(8,128)S(1)}, f32[128,8,512]{2,0,1:T(8,128)}) %tuple.59, (s32[256]{0:T(256)S(1)}, s32[128]{0:T(128)S(1)}, s32[256]{0:T(256)S(1)}, s32[128]{0:T(128)S(1)}, ...), branch_computations={%region_5.5_spmd, %region_6.8_spmd} | conditional | flops 573933568 | bytes 26053720 | solution.py:105
  210.5 2.2 fusion.30
  213.2 1.0 multiply_add_fusion
  214.2 1.4 copy-done.2
  215.5 3.6 conditional.5
  215.6 2.0 fusion.31
  218.1 1.0 multiply_add_fusion.2
  225.5 0.8 dynamic-slice.6
  226.3 1.1 multiply_convert_fusion.2
  228.4 1.4 copy-done.3
  230.1 0.8 fusion.24
  230.9 10.9 %convolution_convert_fusion = bf16[256,7168]{1,0:T(8,128)(2,1)} fusion(bf16[256,1024]{0,1:T(8,128)(2,1)S(1)} %bitcast.45, bf16[1024,7168]{1,0:T(8,128)(2,1)} %param.19), kind=kOutput, calls=%fused_computation.34 | convolution fusion | flops 3759931392 | bytes 18874368 | tf_op jit(solution)/shard_map/dot_general | solution.py:118
  241.8 5.9 %copy.32 = bf16[256,7168]{0,1:T(8,128)(2,1)} copy(bf16[256,7168]{1,0:T(8,128)(2,1)} %convolution_convert_fusion) | data formatting | bytes 7340032
  247.7 149.4 %reduce-scatter.4.cloned.1.call-done = bf16[896,256]{1,0:T(8,128)(2,1)} async-done(((bf16[7168,256]{1,0:T(8,128)(2,1)}), bf16[896,256]{1,0:T(8,128)(2,1)}) %reduce-scatter.4.cloned.1.call-update) | async-done | bytes 458768
  397.1 2.0 copy.33
  (194 shorter events, 49.9 us)
Async XLA Ops:
  6.5 22.1 %copy-start = (bf16[8,128,512]{2,1,0:T(8,128)(2,1)S(1)}, bf16[8,128,512]{2,1,0:T(8,128)(2,1)}, u32[]{:S(2)}) copy-start(bf16[8,128,512]{2,1,0:T(8,128)(2,1)} %param.17) | copy-start | bytes 3145732
  6.5 61.8 %all-gather.3.cloned.1.call-start = ((), (), s32[]{:S(2)}) async-start(), calls=%async_computation.1 | async-start | bytes 5570560 | tf_op jit(solution)/shard_map/all_gather | solution.py:71
  8.5 388.6 %reduce-scatter.4.cloned.1.call-start = ((), (), s32[]{:S(2)}) async-start(), calls=%async_computation.2 | async-start | bytes 4128768
  28.5 1.9 slice-start
  196.4 2.6 copy-start.1
  200.1 1.4 copy-start.2
  210.5 2.6 copy-start.1
  214.2 1.4 copy-start.2
  228.2 1.6 copy-start.3
  228.4 1.7 copy-start.4
Sparse Core Ops, SparseCore 0:
  9.8 58.5 all-gather.2
  247.8 149.2 reduce-scatter.3
where the time goes:
time: 410 us; the launch traced here: 406 us
  waiting for transfers between devices  185 us (45%)
  local copies, waits for them, and re-layouts  67.9 us (17%)
  loops' own time  62 us (15%)
  other arithmetic  36 us (9%)
  matrix products  22.9 us (6%)
  blocking collectives  18.4 us (4%)
  between operations  13.5 us (3%)
    unnamed x3, waiting for transfers between devices  149 us
    another operation x1, loops' own time, shards(): final_state = lax.fori_loop(0, tile_count, tile_step, initial)  61.9 us
    slice x64, local copies, waits for them, and re-layouts, tile_step(): needed = (key_pos[0] <= query_pos[-1]) & (key_seg[-1] >= query_seg[0])  37.2 us
    all_gather x1, waiting for transfers between devices, shards(): latent_rows = lax.all_gather(latents, 'ctx', axis=0, tiled=True)  35.8 us
    all_gather x1, blocking collectives, shards(): lax.all_gather(lat_scale.astype(jnp.bfloat16), 'ctx', axis=0, tiled=True)  18.4 us
    convert_element_type x16, other arithmetic, dequantize(): (latent_rows[:, :LAT].astype(jnp.float32) * scale_rows[:, None]).astype(j...  16.9 us
    slice x16, local copies, waits for them, and re-layouts, dequantize(): return jnp.concatenate([scaled, latent_rows[:, LAT:]], axis=1)  13.5 us
    concatenate x16, other arithmetic, dequantize(): return jnp.concatenate([scaled, latent_rows[:, LAT:]], axis=1)  12.1 us
  transfers between devices with their start and end apart: 2, of which 2 were waited for; matrix products, arithmetic and copies ran while one was open for 1% of the time, Pallas kernels for 0%

commit v1 on v0

v1 whole, which is shorter than its diff:
```python
import functools

import jax
import jax.numpy as jnp
from jax import lax
from jax.experimental import pallas as pl
from jax.experimental.pallas import tpu as pltpu
from jax.sharding import PartitionSpec as P

LAT = 512
NOPE = 128
QDIM = 192
VDIM = 128
TOK = 256
KT = 256
PAIR = 2
NEG = -1e30
EXP_SCALE = float(QDIM) ** -0.5 * 1.4426950408889634


def attention_kernel(
    lens_ref, where_ref, q_ref, uk_ref, deq_ref, uv_ref, out_ref, qf_ref, s_ref, m_ref, l_ref, acc_ref
):
    rows = PAIR * TOK
    c = where_ref[0]
    t0 = c * TOK
    starts = []
    ends = []
    total = jnp.int32(0)
    for k in range(8):
        starts.append(total)
        total = total + lens_ref[k]
        ends.append(total)

    def start_of(t):
        first = jnp.zeros_like(t)
        for k in range(8):
            first = jnp.where(t >= ends[k], ends[k], first)
        return first

    lo_start = start_of(t0)
    hi_start = start_of(t0 + TOK - 1)
    tile_lo = lo_start // KT
    tile_mid = jnp.minimum(jnp.maximum((hi_start + KT - 1) // KT, tile_lo), c)

    for i in range(PAIR):
        q = q_ref[i]
        lat = jnp.dot(q[:, :NOPE], uk_ref[i], preferred_element_type=jnp.float32)
        qf_ref[i * TOK : (i + 1) * TOK, :LAT] = lat.astype(jnp.bfloat16)
        qf_ref[i * TOK : (i + 1) * TOK, LAT:] = q[:, NOPE:]

    m_ref[...] = jnp.full_like(m_ref, NEG)

    def scores(j):
        keys = deq_ref[pl.ds(pl.multiple_of(j * KT, KT), KT), :]
        return lax.dot_general(
            qf_ref[...], keys, (((1,), (1,)), ((), ())), preferred_element_type=jnp.float32
        )

    def put(j, s):
        s_ref[j] = s
        m_ref[...] = jnp.maximum(m_ref[...], jnp.maximum(s[:, :128], s[:, 128:]))

    def masked(j, carry):
        s = scores(j)
        qpos = t0 + lax.broadcasted_iota(jnp.int32, (rows, 1), 0) % TOK
        first = start_of(qpos)
        kpos = j * KT + lax.broadcasted_iota(jnp.int32, (rows, KT), 1)
        put(j, jnp.where((kpos >= first) & (kpos <= qpos), s, NEG))
        return carry

    def plain(j, carry):
        put(j, scores(j))
        return carry

    lax.fori_loop(tile_lo, tile_mid, masked, 0)
    lax.fori_loop(tile_mid, c, plain, 0)
    masked(c, 0)

    pair_lo = tile_lo // 2
    pair_hi = c // 2

    @pl.when(tile_lo % 2 == 1)
    def _():
        s_ref[tile_lo - 1] = jnp.full((rows, KT), NEG, jnp.float32)

    @pl.when(c % 2 == 0)
    def _():
        s_ref[c + 1] = jnp.full((rows, KT), NEG, jnp.float32)

    m = jnp.max(m_ref[...], axis=1, keepdims=True)
    m_ref[...] = jnp.broadcast_to(m, m_ref.shape)
    l_ref[...] = jnp.zeros_like(l_ref)
    acc_ref[...] = jnp.zeros_like(acc_ref)

    def weigh(j, carry):
        top = m_ref[...]
        parts = []
        total = l_ref[...]
        for half in range(2):
            s = s_ref[2 * j + half]
            for lane in range(0, KT, 128):
                p = jnp.exp2((s[:, lane : lane + 128] - top) * EXP_SCALE)
                total = total + p
                parts.append(p.astype(jnp.bfloat16))
        l_ref[...] = total
        p = jnp.concatenate(parts, axis=1)
        values = deq_ref[pl.ds(pl.multiple_of(j * 2 * KT, 2 * KT), 2 * KT), :LAT]
        acc_ref[...] += jnp.dot(p, values, preferred_element_type=jnp.float32)
        return carry

    lax.fori_loop(pair_lo, pair_hi + 1, weigh, 0)
    denominator = jnp.sum(l_ref[...], axis=1, keepdims=True)
    context = (acc_ref[...] / denominator).astype(jnp.bfloat16)
    for i in range(PAIR):
        head = jnp.dot(
            context[i * TOK : (i + 1) * TOK], uv_ref[i], preferred_element_type=jnp.float32
        )
        out_ref[:, i * VDIM : (i + 1) * VDIM] = head.astype(jnp.bfloat16)


def attention(doc_lengths, ctx_index, query, w_uk, deq, w_uv):
    heads = query.shape[0]
    keys = deq.shape[0]
    rows = PAIR * TOK
    return pl.pallas_call(
        attention_kernel,
        out_shape=jax.ShapeDtypeStruct((TOK, heads * VDIM), jnp.bfloat16),
        grid_spec=pltpu.PrefetchScalarGridSpec(
            num_scalar_prefetch=2,
            grid=(heads // PAIR,),
            in_specs=[
                pl.BlockSpec((PAIR, TOK, QDIM), lambda i, a, b: (i, 0, 0)),
                pl.BlockSpec((PAIR, NOPE, LAT), lambda i, a, b: (i, 0, 0)),
                pl.BlockSpec((keys, deq.shape[1]), lambda i, a, b: (0, 0)),
                pl.BlockSpec((PAIR, LAT, VDIM), lambda i, a, b: (i, 0, 0)),
            ],
            out_specs=pl.BlockSpec((TOK, PAIR * VDIM), lambda i, a, b: (0, i)),
            scratch_shapes=[
                pltpu.VMEM((rows, deq.shape[1]), jnp.bfloat16),
                pltpu.VMEM((keys // KT, rows, KT), jnp.float32),
                pltpu.VMEM((rows, 128), jnp.float32),
                pltpu.VMEM((rows, 128), jnp.float32),
                pltpu.VMEM((rows, LAT), jnp.float32),
            ],
        ),
        compiler_params=pltpu.CompilerParams(vmem_limit_bytes=40 << 20),
        name="attention",
    )(doc_lengths, ctx_index, query, w_uk, deq, w_uv)


def shards(query, latents, lat_scale, doc_lengths, w_uk, w_uv, w_o):
    ctx_index = lax.axis_index("ctx").astype(jnp.int32).reshape(1)
    scaled = (latents[:, :LAT].astype(jnp.float32) * lat_scale[:, None]).astype(jnp.bfloat16)
    deq = jnp.concatenate([scaled, latents[:, LAT:]], axis=1)
    deq = lax.all_gather(deq, "ctx", axis=0, tiled=True)
    by_head = jnp.transpose(query, (1, 0, 2))
    head_out = attention(doc_lengths, ctx_index, by_head, w_uk, deq, w_uv)
    partial_value = jnp.dot(head_out, w_o, preferred_element_type=jnp.float32)
    return lax.psum_scatter(
        partial_value.astype(jnp.bfloat16), "head", scatter_dimension=1, tiled=True
    )


def solution(mesh):
    placed = (
        P("ctx", "head", None),
        P("ctx", None),
        P("ctx"),
        P(),
        P("head", None, None),
        P("head", None, None),
        P("head", None),
    )
    return jax.shard_map(
        shards, mesh=mesh, in_specs=placed, out_specs=P("ctx", "head"), check_vma=False
    )
```

time: 410 us -> 193 us (0.47)
  loops' own time: 62 us -> 0 us
  local copies, waits for them, and re-layouts: 67.9 us -> 16.9 us
  waiting for transfers between devices: 185 us -> 136 us
  other arithmetic: 36 us -> 1.54 us
  blocking collectives: 18.4 us -> 0 us
  Pallas kernels: 0 us -> 13.3 us
  matrix products: 22.9 us -> 10.6 us
    unnamed x3, waiting for transfers between devices: 149 us -> 78.4 us
    another operation x33 -> x0, loops' own time: 62 us -> none  [the longest x1 61.9 us: shards(): final_state = lax.fori_loop(0, tile_count, tile_step, initial)]
    slice x82 -> x2, local copies, waits for them, and re-layouts: 50.7 us -> 1.73 us  [the longest x1 0.97 us: shards(): latents[:, :LAT].astype(jnp.float32) * lat_scale[:, None]]
    all_gather x1, waiting for transfers between devices: 35.8 us -> 57.2 us  [shards(): deq = lax.all_gather(deq, 'ctx', axis=0, tiled=True)]
    all_gather x1 -> x0, blocking collectives: 18.4 us -> none  [shards(): lax.all_gather(lat_scale.astype(jnp.bfloat16), 'ctx', axis=0, tiled=True)]
    convert_element_type x20 -> x1, other arithmetic: 18 us -> 0.79 us  [shards(): (latents[:, :LAT].astype(jnp.float32) * lat_scale[:, None]).astype(jnp.bf...]
    concatenate x17 -> x1, other arithmetic: 14.2 us -> 0.75 us  [shards(): deq = jnp.concatenate([scaled, latents[:, LAT:]], axis=1)]
    pallas_call x0 -> x1, Pallas kernels: none -> 13.3 us  [attention(): pl.pallas_call(attention_kernel, out_shape=jax.ShapeDtypeStruct((TOK, hea...]
where the time goes in v1:
time: 193 us; the launch traced here: 191 us
  waiting for transfers between devices  136 us (70%)
  local copies, waits for them, and re-layouts  16.9 us (9%)
  between operations  13.4 us (7%)
  Pallas kernels  13.3 us (7%)
  matrix products  10.6 us (5%)
    unnamed x3, waiting for transfers between devices  78.4 us
    all_gather x1, waiting for transfers between devices, shards(): deq = lax.all_gather(deq, 'ctx', axis=0, tiled=True)  57.2 us
    unnamed x13, local copies, waits for them, and re-layouts  15.2 us
    pallas_call x1, Pallas kernels, attention(): pl.pallas_call(attention_kernel, out_shape=jax.ShapeDtypeStruct((TOK, hea...  13.3 us
    dot_general x1, matrix products, shards(): partial_value = jnp.dot(head_out, w_o, preferred_element_type=jnp.float32)  10.6 us
  transfers between devices with their start and end apart: 2, of which 2 were waited for; matrix products, arithmetic and copies ran while one was open for 1% of the time, Pallas kernels for 0%

profile of v1, /device:TPU:70, one launch (start us, length us, event | category | flops | bytes accessed | tf_op | source)
XLA Modules:
  0.0 191.4 jit_solution(14957282104494216121)
XLA Ops:
  6.5 0.0 all-gather.2.cloned.1.call-start
  6.5 0.8 slice.7
  7.3 1.0 slice.6
  8.3 0.1 copy.17
  8.4 0.1 copy.16
  8.5 0.8 multiply_convert_fusion
  9.3 0.8 pad_maximum_fusion
  10.1 0.0 all-gather.2.cloned.1.call-update
  10.1 0.0 reduce-scatter.4.cloned.1.call-start
  10.2 1.4 copy.11
  11.6 57.2 %all-gather.2.cloned.1.call-done.deq_ref = bf16[4096,576]{1,0:T(8,128)(2,1)} async-done(((bf16[256,576]{1,0:T(8,128)(2,1)}), bf16[4096,576]{1,0:T(8,128)(2,1)}) %all-gather.2.cloned.1.call-update) | async-done | bytes 4718608 | tf_op jit(solution)/shard_map/all_gather | solution.py:156
  68.8 0.0 copy-start
  68.8 2.5 %copy-done = bf16[4096,576]{1,0:T(8,128)(2,1)S(1)} copy-done((bf16[4096,576]{1,0:T(8,128)(2,1)S(1)}, bf16[4096,576]{1,0:T(8,128)(2,1)}, u32[]{:S(2)}) %copy-start) | copy-done | bytes 4718616
  71.3 0.0 copy-start.1
  71.3 1.2 copy-done.1
  72.5 0.0 copy-start.2
  72.5 1.2 copy-done.2
  73.7 0.0 copy-start.3
  73.7 0.7 copy-done.3
  74.4 13.3 %attention.1 = bf16[256,1024]{1,0:T(8,128)(2,1)S(1)} custom-call(s32[8]{0:T(128)S(1)} %copy-done.3, s32[1]{0:T(128)} %bitcast.where_ref, bf16[8,256,192]{2,1,0:T(8,128)(2,1)S(1)} %bitcast.6, bf16[8,128,512]{2,1,0:T(8,128)(2,1)S(1)} %copy-done.1, bf16[4096,576]{1,0:T(8,128)(2,1)S(1)} %copy-done, bf16[8,512,128]{2,1,0:T(8,128)(2,1)S(1)} %copy-done.2), custom_call_target="tpu_custom_call" | custom-call | tf_op jit(solution)/shard_map/attention/pallas_call | solution.py:126
  87.7 10.6 %convolution_convert_fusion = bf16[256,7168]{1,0:T(8,128)(2,1)} fusion(bf16[256,1024]{1,0:T(8,128)(2,1)S(1)} %attention.1, bf16[1024,7168]{1,0:T(8,128)(2,1)} %param.13), kind=kOutput, calls=%fused_computation | convolution fusion | flops 3759931392 | bytes 18874368 | tf_op jit(solution)/shard_map/dot_general | solution.py:159
  98.3 5.9 %copy.14 = bf16[256,7168]{0,1:T(8,128)(2,1)} copy(bf16[256,7168]{1,0:T(8,128)(2,1)} %convolution_convert_fusion) | data formatting | bytes 7340032
  104.2 0.0 reduce-scatter.4.cloned.1.call-update
  104.3 78.3 %reduce-scatter.4.cloned.1.call-done = bf16[896,256]{1,0:T(8,128)(2,1)} async-done(((bf16[7168,256]{1,0:T(8,128)(2,1)}), bf16[896,256]{1,0:T(8,128)(2,1)}) %reduce-scatter.4.cloned.1.call-update) | async-done | bytes 458768
  182.6 2.0 %copy.15 = bf16[256,896]{1,0:T(8,128)(2,1)} copy(bf16[256,896]{0,1:T(8,128)(2,1)} %bitcast.8) | data formatting | bytes 917504
Async XLA Ops:
  6.5 62.2 %all-gather.2.cloned.1.call-start = ((), (), s32[]{:S(2)}) async-start(), calls=%async_computation.1 | async-start | bytes 5570560 | tf_op jit(solution)/shard_map/all_gather | solution.py:156
  10.1 172.5 %reduce-scatter.4.cloned.1.call-start = ((), (), s32[]{:S(2)}) async-start(), calls=%async_computation.2 | async-start | bytes 4128768
  68.8 2.5 %copy-start = (bf16[4096,576]{1,0:T(8,128)(2,1)S(1)}, bf16[4096,576]{1,0:T(8,128)(2,1)}, u32[]{:S(2)}) copy-start(bf16[4096,576]{1,0:T(8,128)(2,1)} %all-gather.2.cloned.1.call-done.deq_ref) | copy-start | bytes 14155780
  71.3 1.2 copy-start.1
  72.5 1.2 copy-start.2
  73.7 0.7 copy-start.3
Sparse Core Ops, SparseCore 0:
  10.2 58.5 all-gather.1
  104.4 78.1 reduce-scatter.3

commit v2 on v1

--- a/solution.py
+++ b/solution.py
@@ -1,5 +1,3 @@
-import functools
-
 import jax
 import jax.numpy as jnp
 from jax import lax
@@ -15,6 +13,7 @@
 KT = 256
 PAIR = 2
 NEG = -1e30
+MESH = pl.DeviceIdType.MESH
 EXP_SCALE = float(QDIM) ** -0.5 * 1.4426950408889634
 
 
@@ -149,6 +148,173 @@
     )(doc_lengths, ctx_index, query, w_uk, deq, w_uv)
 
 
+def reduce_kernel(
+    x_ref, w_ref, out_ref, wbuf, own, zrecv, y1recv, y2recv, ysecond1, ysecond2, zlast,
+    wsem, zsend, zgot, y1send, y1got, y2send, y2got, s1send, s1got, s2send, s2got, lsend, lgot,
+):
+    cols = out_ref.shape[1]
+    half = out_ref.shape[0] // 2
+    quarter = half // 2
+    me = lax.axis_index("head")
+    y = lax.rem(me, 4)
+    z = me // 4
+    up = z * 4 + lax.rem(y + 1, 4)
+    down = z * 4 + lax.rem(y + 3, 4)
+    across = (1 - z) * 4 + y
+    blocks = ((2, 0), (2, 1), (1, 0), (3, 0), (1, 1), (3, 1), (0, 0), (0, 1))
+    slot = {key: k for k, key in enumerate(blocks)}
+    first = pl.ds(0, half)
+    second = pl.ds(half, half)
+
+    def fetch(k):
+        shift, mine = blocks[k]
+        plane = z if mine else 1 - z
+        start = pl.multiple_of((plane * 4 + lax.rem(y + shift, 4)) * cols, 128)
+        return pltpu.make_async_copy(w_ref.at[:, pl.ds(start, cols)], wbuf.at[k], wsem.at[k])
+
+    def send(src, dst, ssem, rsem, target):
+        return pltpu.make_async_remote_copy(
+            src_ref=src, dst_ref=dst, send_sem=ssem, recv_sem=rsem,
+            device_id={"head": target}, device_id_type=MESH,
+        )
+
+    for k in range(8):
+        fetch(k).start()
+    barrier = pltpu.get_barrier_semaphore()
+    for target in (up, down, across):
+        pl.semaphore_signal(barrier, inc=1, device_id={"head": target}, device_id_type=MESH)
+    pl.semaphore_wait(barrier, 3)
+
+    pending = []
+
+    def go(copy):
+        copy.start()
+        pending.append(copy)
+
+    def across_copy(i, k):
+        return send(own.at[k, first], zrecv.at[i], zsend.at[i], zgot.at[i], across)
+
+    def step1(k, base, buf, ssem, rsem, i):
+        go(send(own.at[k, pl.ds(base, quarter)], buf.at[i], ssem.at[i], rsem.at[i], up))
+        go(
+            send(
+                own.at[k, pl.ds(base + quarter, quarter)],
+                buf.at[i + 1], ssem.at[i + 1], rsem.at[i + 1], down,
+            )
+        )
+
+    across_order = (2, 1, 3, 0)
+    across_copies = {}
+
+    def compute(k):
+        fetch(k).wait()
+        own[k] = jnp.dot(x_ref[...], wbuf[k], preferred_element_type=jnp.float32).astype(
+            jnp.bfloat16
+        )
+        shift, mine = blocks[k]
+        if not mine:
+            i = across_order.index(shift)
+            across_copies[i] = across_copy(i, k)
+            go(across_copies[i])
+        if shift == 2:
+            step1(k, half, y1recv, y1send, y1got, 2 * mine)
+
+    def add_rows(k, rows, *terms):
+        total = own[k, rows].astype(jnp.float32)
+        for term in terms:
+            total = total + term.astype(jnp.float32)
+        return total
+
+    copies = {}
+
+    def y_first_step2(mine):
+        for side, (shift, target, offset) in enumerate(((1, up, 0), (3, down, quarter))):
+            k = slot[(shift, mine)]
+            i = 2 * mine + side
+            rows = pl.ds(half + offset, quarter)
+            send(
+                own.at[0, pl.ds(0, quarter)], y1recv.at[i], y1send.at[i], y1got.at[i], target
+            ).wait_recv()
+            own[k, rows] = add_rows(k, rows, y1recv[i]).astype(jnp.bfloat16)
+            go(send(own.at[k, second], y2recv.at[i], y2send.at[i], y2got.at[i], target))
+
+    def got(buf, i, ssem, rsem, rows):
+        send(own.at[0, pl.ds(0, rows)], buf.at[i], ssem.at[i], rsem.at[i], across).wait_recv()
+
+    for k in range(6):
+        compute(k)
+    y_first_step2(0)
+    for k in range(6, 8):
+        compute(k)
+    y_first_step2(1)
+
+    got(zrecv, 0, zsend, zgot, half)
+    k = slot[(2, 1)]
+    own[k, first] = add_rows(k, first, zrecv[0]).astype(jnp.bfloat16)
+    step1(k, 0, ysecond1, s1send, s1got, 0)
+
+    got(y2recv, 0, y2send, y2got, half)
+    got(y2recv, 1, y2send, y2got, half)
+    k = slot[(0, 0)]
+    own[k, second] = add_rows(k, second, y2recv[0], y2recv[1]).astype(jnp.bfloat16)
+    go(send(own.at[k, second], zlast.at[0], lsend.at[0], lgot.at[0], across))
+
+    for side, (shift, target, offset) in enumerate(((1, up, 0), (3, down, quarter))):
+        k = slot[(shift, 1)]
+        got(zrecv, 1 + side, zsend, zgot, half)
+        got(ysecond1, side, s1send, s1got, quarter)
+        own[k, first] = add_rows(k, first, zrecv[1 + side]).astype(jnp.bfloat16)
+        rows = pl.ds(offset, quarter)
+        own[k, rows] = add_rows(k, rows, ysecond1[side]).astype(jnp.bfloat16)
+        go(send(own.at[k, first], ysecond2.at[side], s2send.at[side], s2got.at[side], target))
+
+    k = slot[(0, 1)]
+    got(y2recv, 2, y2send, y2got, half)
+    got(y2recv, 3, y2send, y2got, half)
+    got(zlast, 0, lsend, lgot, half)
+    out_ref[second] = add_rows(k, second, y2recv[2], y2recv[3], zlast[0]).astype(jnp.bfloat16)
+    got(zrecv, 3, zsend, zgot, half)
+    got(ysecond2, 0, s2send, s2got, half)
+    got(ysecond2, 1, s2send, s2got, half)
+    out_ref[first] = add_rows(k, first, zrecv[3], ysecond2[0], ysecond2[1]).astype(jnp.bfloat16)
+    for copy in pending:
+        copy.wait_send()
+
+
+def project_and_reduce(head_out, w_o):
+    rows, inner = head_out.shape
+    cols = w_o.shape[1] // 8
+    half = rows // 2
+    dma = pltpu.SemaphoreType.DMA
+    return pl.pallas_call(
+        reduce_kernel,
+        out_shape=jax.ShapeDtypeStruct((rows, cols), jnp.bfloat16),
+        in_specs=[pl.BlockSpec(memory_space=pltpu.VMEM), pl.BlockSpec(memory_space=pl.ANY)],
+        out_specs=pl.BlockSpec(memory_space=pltpu.VMEM),
+        scratch_shapes=[
+            pltpu.VMEM((8, inner, cols), jnp.bfloat16),
+            pltpu.VMEM((8, rows, cols), jnp.bfloat16),
+            pltpu.VMEM((4, half, cols), jnp.bfloat16),
+            pltpu.VMEM((4, half // 2, cols), jnp.bfloat16),
+            pltpu.VMEM((4, half, cols), jnp.bfloat16),
+            pltpu.VMEM((2, half // 2, cols), jnp.bfloat16),
+            pltpu.VMEM((2, half, cols), jnp.bfloat16),
+            pltpu.VMEM((1, half, cols), jnp.bfloat16),
+            dma((8,)),
+            dma((4,)), dma((4,)),
+            dma((4,)), dma((4,)),
+            dma((4,)), dma((4,)),
+            dma((2,)), dma((2,)),
+            dma((2,)), dma((2,)),
+            dma((1,)), dma((1,)),
+        ],
+        compiler_params=pltpu.CompilerParams(
+            collective_id=0, has_side_effects=True, vmem_limit_bytes=40 << 20
+        ),
+        name="project_and_reduce",
+    )(head_out, w_o)
+
+
 def shards(query, latents, lat_scale, doc_lengths, w_uk, w_uv, w_o):
     ctx_index = lax.axis_index("ctx").astype(jnp.int32).reshape(1)
     scaled = (latents[:, :LAT].astype(jnp.float32) * lat_scale[:, None]).astype(jnp.bfloat16)
@@ -156,10 +322,7 @@
     deq = lax.all_gather(deq, "ctx", axis=0, tiled=True)
     by_head = jnp.transpose(query, (1, 0, 2))
     head_out = attention(doc_lengths, ctx_index, by_head, w_uk, deq, w_uv)
-    partial_value = jnp.dot(head_out, w_o, preferred_element_type=jnp.float32)
-    return lax.psum_scatter(
-        partial_value.astype(jnp.bfloat16), "head", scatter_dimension=1, tiled=True
-    )
+    return project_and_reduce(head_out, w_o)
 
 
 def solution(mesh):

time: 193 us -> 150 us (0.78)
  the two profiles are of different devices: /device:TPU:70 before, /device:TPU:67 now
where the time goes in v2:
time: 150 us; the launch traced here: 148 us
  Pallas kernels  65.2 us (43%)
  waiting for transfers between devices  57.7 us (38%)
  between operations  13.4 us (9%)
  local copies, waits for them, and re-layouts  9.78 us (7%)
  other arithmetic  1.54 us (1%)
    all_gather x1, waiting for transfers between devices, shards(): deq = lax.all_gather(deq, 'ctx', axis=0, tiled=True)  57.7 us
    pallas_call x1, Pallas kernels, attention(): pl.pallas_call(attention_kernel, out_shape=jax.ShapeDtypeStruct((TOK, hea...  34.6 us
    pallas_call x1, Pallas kernels, project_and_reduce(): pl.pallas_call(reduce_kernel, out_shape=jax.ShapeDtypeStruct((rows, cols)...  30.6 us
    unnamed x12, local copies, waits for them, and re-layouts  8.05 us
  transfers between devices with their start and end apart: 1, of which 1 were waited for; matrix products, arithmetic and copies ran while one was open for 1% of the time, Pallas kernels for 0%

profile of v2, /device:TPU:67, one launch (start us, length us, event | category | flops | bytes accessed | tf_op | source)
XLA Modules:
  0.0 147.7 jit_solution(9264842207187385489)
XLA Ops:
  6.5 0.0 all-gather.2.cloned.1.call-start
  6.5 0.8 slice.7
  7.3 1.0 slice.6
  8.3 0.1 copy.12
  8.4 0.1 copy.11
  8.5 0.8 multiply_convert_fusion
  9.3 0.8 pad_maximum_fusion
  10.1 0.0 all-gather.2.cloned.1.call-update
  10.1 1.4 copy.8
  11.6 57.7 %all-gather.2.cloned.1.call-done.deq_ref = bf16[4096,576]{1,0:T(8,128)(2,1)} async-done(((bf16[256,576]{1,0:T(8,128)(2,1)}), bf16[4096,576]{1,0:T(8,128)(2,1)}) %all-gather.2.cloned.1.call-update) | async-done | bytes 4718608 | tf_op jit(solution)/shard_map/all_gather | solution.py:322
  69.3 0.0 copy-start
  69.3 2.5 %copy-done = bf16[4096,576]{1,0:T(8,128)(2,1)S(1)} copy-done((bf16[4096,576]{1,0:T(8,128)(2,1)S(1)}, bf16[4096,576]{1,0:T(8,128)(2,1)}, u32[]{:S(2)}) %copy-start) | copy-done | bytes 4718616
  71.7 0.0 copy-start.1
  71.7 1.2 copy-done.1
  73.0 0.0 copy-start.2
  73.0 1.2 copy-done.2
  74.2 0.0 copy-start.3
  74.2 0.7 copy-done.3
  74.9 34.6 %attention.1.x_ref = bf16[256,1024]{1,0:T(8,128)(2,1)S(1)} custom-call(s32[8]{0:T(128)S(1)} %copy-done.3, s32[1]{0:T(128)} %bitcast.where_ref, bf16[8,256,192]{2,1,0:T(8,128)(2,1)S(1)} %bitcast.2, bf16[8,128,512]{2,1,0:T(8,128)(2,1)S(1)} %copy-done.1, bf16[4096,576]{1,0:T(8,128)(2,1)S(1)} %copy-done, bf16[8,512,128]{2,1,0:T(8,128)(2,1)S(1)} %copy-done.2), custom_call_target="tpu_custom_call" | custom-call | tf_op jit(solution)/shard_map/attention/pallas_call | solution.py:125
  109.5 30.6 %project_and_reduce.1 = bf16[256,896]{1,0:T(8,128)(2,1)S(1)} custom-call(bf16[256,1024]{1,0:T(8,128)(2,1)S(1)} %attention.1.x_ref, bf16[1024,7168]{1,0:T(8,128)(2,1)} %w_ref.1), custom_call_target="tpu_custom_call" | custom-call | tf_op jit(solution)/shard_map/project_and_reduce/pallas_call | solution.py:289
  140.0 0.8 copy.14
Async XLA Ops:
  6.5 62.7 %all-gather.2.cloned.1.call-start = ((), (), s32[]{:S(2)}) async-start(), calls=%async_computation | async-start | bytes 5570560 | tf_op jit(solution)/shard_map/all_gather | solution.py:322
  69.3 2.5 %copy-start = (bf16[4096,576]{1,0:T(8,128)(2,1)S(1)}, bf16[4096,576]{1,0:T(8,128)(2,1)}, u32[]{:S(2)}) copy-start(bf16[4096,576]{1,0:T(8,128)(2,1)} %all-gather.2.cloned.1.call-done.deq_ref) | copy-start | bytes 14155780
  71.7 1.2 copy-start.1
  73.0 1.2 copy-start.2
  74.2 0.7 copy-start.3
Sparse Core Ops, SparseCore 0:
  10.2 58.9 all-gather.1

commit v3 on v2

--- a/solution.py
+++ b/solution.py
@@ -11,141 +11,129 @@
 VDIM = 128
 TOK = 256
 KT = 256
-PAIR = 2
+GROUP = 4
+PER = 4
 NEG = -1e30
 MESH = pl.DeviceIdType.MESH
 EXP_SCALE = float(QDIM) ** -0.5 * 1.4426950408889634
 
 
-def attention_kernel(
-    lens_ref, where_ref, q_ref, uk_ref, deq_ref, uv_ref, out_ref, qf_ref, s_ref, m_ref, l_ref, acc_ref
-):
-    rows = PAIR * TOK
-    c = where_ref[0]
-    t0 = c * TOK
-    starts = []
+def attention_kernel(lens_ref, qf_ref, keys_ref, uv_ref, out_ref, s_ref, m_ref, l_ref, acc_ref):
+    rows = m_ref.shape[0]
+    group = rows // TOK
+    ctx = lax.axis_index("ctx")
+    t0 = ctx * TOK
     ends = []
     total = jnp.int32(0)
-    for k in range(8):
-        starts.append(total)
+    for k in range(lens_ref.shape[0]):
         total = total + lens_ref[k]
         ends.append(total)
 
     def start_of(t):
         first = jnp.zeros_like(t)
-        for k in range(8):
-            first = jnp.where(t >= ends[k], ends[k], first)
+        for end in ends:
+            first = jnp.where(t >= end, end, first)
         return first
 
-    lo_start = start_of(t0)
-    hi_start = start_of(t0 + TOK - 1)
-    tile_lo = lo_start // KT
-    tile_mid = jnp.minimum(jnp.maximum((hi_start + KT - 1) // KT, tile_lo), c)
-
-    for i in range(PAIR):
-        q = q_ref[i]
-        lat = jnp.dot(q[:, :NOPE], uk_ref[i], preferred_element_type=jnp.float32)
-        qf_ref[i * TOK : (i + 1) * TOK, :LAT] = lat.astype(jnp.bfloat16)
-        qf_ref[i * TOK : (i + 1) * TOK, LAT:] = q[:, NOPE:]
-
-    m_ref[...] = jnp.full_like(m_ref, NEG)
-
-    def scores(j):
-        keys = deq_ref[pl.ds(pl.multiple_of(j * KT, KT), KT), :]
-        return lax.dot_general(
-            qf_ref[...], keys, (((1,), (1,)), ((), ())), preferred_element_type=jnp.float32
-        )
-
-    def put(j, s):
-        s_ref[j] = s
-        m_ref[...] = jnp.maximum(m_ref[...], jnp.maximum(s[:, :128], s[:, 128:]))
-
-    def masked(j, carry):
-        s = scores(j)
-        qpos = t0 + lax.broadcasted_iota(jnp.int32, (rows, 1), 0) % TOK
-        first = start_of(qpos)
-        kpos = j * KT + lax.broadcasted_iota(jnp.int32, (rows, KT), 1)
-        put(j, jnp.where((kpos >= first) & (kpos <= qpos), s, NEG))
+    tile_lo = start_of(t0) // KT
+    tile_mid = jnp.clip((start_of(t0 + TOK - 1) + KT - 1) // KT, tile_lo, ctx)
+    chunk_lo = tile_lo // PER
+    chunk_hi = ctx // PER
+
+    def one_group(g, carry):
+        base = pl.multiple_of(g * rows, rows)
+        m_ref[...] = jnp.full_like(m_ref, NEG)
+
+        def scores(j):
+            keys = keys_ref[pl.ds(pl.multiple_of(j * KT, KT), KT), :]
+            return lax.dot_general(
+                qf_ref[pl.ds(base, rows), :],
+                keys,
+                (((1,), (1,)), ((), ())),
+                preferred_element_type=jnp.float32,
+            )
+
+        def put(j, s):
+            s_ref[j] = s
+            m_ref[...] = jnp.maximum(m_ref[...], jnp.maximum(s[:, :128], s[:, 128:]))
+
+        def masked(j, carry):
+            s = scores(j)
+            qpos = t0 + lax.broadcasted_iota(jnp.int32, (rows, 1), 0) % TOK
+            first = start_of(qpos)
+            kpos = j * KT + lax.broadcasted_iota(jnp.int32, (rows, KT), 1)
+            put(j, jnp.where((kpos >= first) & (kpos <= qpos), s, NEG))
+            return carry
+
+        def plain(j, carry):
+            put(j, scores(j))
+            return carry
+
+        def clear(j, carry):
+            s_ref[j] = jnp.full((rows, KT), NEG, jnp.float32)
+            return carry
+
+        lax.fori_loop(chunk_lo * PER, tile_lo, clear, 0)
+        lax.fori_loop(tile_lo, tile_mid, masked, 0)
+        lax.fori_loop(tile_mid, ctx, plain, 0)
+        masked(ctx, 0)
+        lax.fori_loop(ctx + 1, (chunk_hi + 1) * PER, clear, 0)
+
+        m = jnp.max(m_ref[...], axis=1, keepdims=True)
+        m_ref[...] = jnp.broadcast_to(m, m_ref.shape)
+        l_ref[...] = jnp.zeros_like(l_ref)
+        acc_ref[...] = jnp.zeros_like(acc_ref)
+
+        def weigh(j, carry):
+            top = m_ref[...]
+            parts = []
+            total = l_ref[...]
+            for tile in range(PER):
+                s = s_ref[PER * j + tile]
+                for lane in range(0, KT, 128):
+                    p = jnp.exp2((s[:, lane : lane + 128] - top) * EXP_SCALE)
+                    total = total + p
+                    parts.append(p.astype(jnp.bfloat16))
+            l_ref[...] = total
+            p = jnp.concatenate(parts, axis=1)
+            chunk = PER * KT
+            values = keys_ref[pl.ds(pl.multiple_of(j * chunk, chunk), chunk), :LAT]
+            acc_ref[...] += jnp.dot(p, values, preferred_element_type=jnp.float32)
+            return carry
+
+        lax.fori_loop(chunk_lo, chunk_hi + 1, weigh, 0)
+        denominator = jnp.sum(l_ref[...], axis=1, keepdims=True)
+        context = (acc_ref[...] / denominator).astype(jnp.bfloat16)
+        for i in range(group):
+            h = g * group + i
+            head = jnp.dot(
+                context[i * TOK : (i + 1) * TOK], uv_ref[h], preferred_element_type=jnp.float32
+            )
+            out_ref[:, pl.ds(pl.multiple_of(h * VDIM, VDIM), VDIM)] = head.astype(jnp.bfloat16)
         return carry
 
-    def plain(j, carry):
-        put(j, scores(j))
-        return carry
-
-    lax.fori_loop(tile_lo, tile_mid, masked, 0)
-    lax.fori_loop(tile_mid, c, plain, 0)
-    masked(c, 0)
-
-    pair_lo = tile_lo // 2
-    pair_hi = c // 2
-
-    @pl.when(tile_lo % 2 == 1)
-    def _():
-        s_ref[tile_lo - 1] = jnp.full((rows, KT), NEG, jnp.float32)
-
-    @pl.when(c % 2 == 0)
-    def _():
-        s_ref[c + 1] = jnp.full((rows, KT), NEG, jnp.float32)
-
-    m = jnp.max(m_ref[...], axis=1, keepdims=True)
-    m_ref[...] = jnp.broadcast_to(m, m_ref.shape)
-    l_ref[...] = jnp.zeros_like(l_ref)
-    acc_ref[...] = jnp.zeros_like(acc_ref)
-
-    def weigh(j, carry):
-        top = m_ref[...]
-        parts = []
-        total = l_ref[...]
-        for half in range(2):
-            s = s_ref[2 * j + half]
-            for lane in range(0, KT, 128):
-                p = jnp.exp2((s[:, lane : lane + 128] - top) * EXP_SCALE)
-                total = total + p
-                parts.append(p.astype(jnp.bfloat16))
-        l_ref[...] = total
-        p = jnp.concatenate(parts, axis=1)
-        values = deq_ref[pl.ds(pl.multiple_of(j * 2 * KT, 2 * KT), 2 * KT), :LAT]
-        acc_ref[...] += jnp.dot(p, values, preferred_element_type=jnp.float32)
-        return carry
-
-    lax.fori_loop(pair_lo, pair_hi + 1, weigh, 0)
-    denominator = jnp.sum(l_ref[...], axis=1, keepdims=True)
-    context = (acc_ref[...] / denominator).astype(jnp.bfloat16)
-    for i in range(PAIR):
-        head = jnp.dot(
-            context[i * TOK : (i + 1) * TOK], uv_ref[i], preferred_element_type=jnp.float32
-        )
-        out_ref[:, i * VDIM : (i + 1) * VDIM] = head.astype(jnp.bfloat16)
-
-
-def attention(doc_lengths, ctx_index, query, w_uk, deq, w_uv):
-    heads = query.shape[0]
-    keys = deq.shape[0]
-    rows = PAIR * TOK
+    lax.fori_loop(0, qf_ref.shape[0] // rows, one_group, 0)
+
+
+def attention(doc_lengths, query_full, keys, w_uv):
+    heads = w_uv.shape[0]
+    length = keys.shape[0]
+    rows = GROUP * TOK
+    vmem = pl.BlockSpec(memory_space=pltpu.VMEM)
     return pl.pallas_call(
         attention_kernel,
         out_shape=jax.ShapeDtypeStruct((TOK, heads * VDIM), jnp.bfloat16),
-        grid_spec=pltpu.PrefetchScalarGridSpec(
-            num_scalar_prefetch=2,
-            grid=(heads // PAIR,),
-            in_specs=[
-                pl.BlockSpec((PAIR, TOK, QDIM), lambda i, a, b: (i, 0, 0)),
-                pl.BlockSpec((PAIR, NOPE, LAT), lambda i, a, b: (i, 0, 0)),
-                pl.BlockSpec((keys, deq.shape[1]), lambda i, a, b: (0, 0)),
-                pl.BlockSpec((PAIR, LAT, VDIM), lambda i, a, b: (i, 0, 0)),
-            ],
-            out_specs=pl.BlockSpec((TOK, PAIR * VDIM), lambda i, a, b: (0, i)),
-            scratch_shapes=[
-                pltpu.VMEM((rows, deq.shape[1]), jnp.bfloat16),
-                pltpu.VMEM((keys // KT, rows, KT), jnp.float32),
-                pltpu.VMEM((rows, 128), jnp.float32),
-                pltpu.VMEM((rows, 128), jnp.float32),
-                pltpu.VMEM((rows, LAT), jnp.float32),
-            ],
-        ),
-        compiler_params=pltpu.CompilerParams(vmem_limit_bytes=40 << 20),
+        in_specs=[pl.BlockSpec(memory_space=pltpu.SMEM), vmem, vmem, vmem],
+        out_specs=vmem,
+        scratch_shapes=[
+            pltpu.VMEM((length // KT, rows, KT), jnp.float32),
+            pltpu.VMEM((rows, 128), jnp.float32),
+            pltpu.VMEM((rows, 128), jnp.float32),
+            pltpu.VMEM((rows, LAT), jnp.float32),
+        ],
+        compiler_params=pltpu.CompilerParams(vmem_limit_bytes=44 << 20),
         name="attention",
-    )(doc_lengths, ctx_index, query, w_uk, deq, w_uv)
+    )(doc_lengths, query_full, keys, w_uv)
 
 
 def reduce_kernel(
@@ -315,13 +303,216 @@
     )(head_out, w_o)
 
 
+def gather_kernel(
+    q_ref, latents_ref, scale_ref, uk_ref, keys_ref, qf_ref,
+    zsend, zgot, x1send, x1got, x2send, x2got, y1send, y1got, y2send, y2got, csend, cgot,
+):
+    rows = latents_ref.shape[0]
+    direct = rows // 2
+    part = (rows - direct) // 4
+    ctx = lax.axis_index("ctx")
+    head = lax.axis_index("head")
+    core = lax.rem(ctx, 2)
+    x = lax.rem(ctx // 2, 4)
+    hi = ctx // 8
+    y = lax.rem(head, 4)
+    lo = head // 4
+    x_up, x_down, x_far = lax.rem(x + 1, 4), lax.rem(x + 3, 4), lax.rem(x + 2, 4)
+    y_up, y_down, y_far = lax.rem(y + 1, 4), lax.rem(y + 3, 4), lax.rem(y + 2, 4)
+    planes = (hi * 4, (1 - hi) * 4)
+
+    def place(a, b, c, d, e):
+        return {"ctx": a * 8 + b * 2 + c, "head": d * 4 + e}
+
+    to_x = (place(hi, x_up, core, lo, y), place(hi, x_down, core, lo, y))
+    to_y = (place(hi, x, core, lo, y_up), place(hi, x, core, lo, y_down))
+    to_z = place(1 - hi, x, core, 1 - lo, y)
+    to_core = place(hi, x, 1 - core, lo, y)
+
+    def strip(index):
+        return pl.ds(pl.multiple_of(direct + index * part, 16), part)
+
+    def strip_half(index, which):
+        return pl.ds(pl.multiple_of(direct + index * part + which * (part // 2), 16), part // 2)
+
+    sets = (strip(y), pl.ds(0, direct))
+    set_halves = (
+        (strip_half(y, 0), strip_half(y, 1)),
+        (pl.ds(0, direct // 2), pl.ds(direct // 2, direct // 2)),
+    )
+
+    def copy(src, dst, ssem, rsem, target):
+        return pltpu.make_async_remote_copy(
+            src_ref=src, dst_ref=dst, send_sem=ssem, recv_sem=rsem,
+            device_id=target, device_id_type=MESH,
+        )
+
+    pending = []
+
+    def go(ref, ssem, rsem, target):
+        one = copy(ref, ref, ssem, rsem, target)
+        one.start()
+        pending.append(one)
+
+    def got(ref, ssem, rsem):
+        copy(ref, ref, ssem, rsem, to_core).wait_recv()
+
+    barrier = pltpu.get_barrier_semaphore()
+    for target in (*to_x, *to_y, to_z, to_core):
+        pl.semaphore_signal(barrier, inc=1, device_id=target, device_id_type=MESH)
+
+    eye = lax.broadcasted_iota(jnp.int32, (rows, rows), 0) == lax.broadcasted_iota(
+        jnp.int32, (rows, rows), 1
+    )
+    column = jnp.sum(jnp.where(eye, scale_ref[...], 0.0), axis=1, keepdims=True)
+    mine = planes[0] + x
+    latent = latents_ref[...]
+    keys_ref[mine, core, :, :LAT] = (latent[:, :LAT].astype(jnp.float32) * column).astype(
+        jnp.bfloat16
+    )
+    keys_ref[mine, core, :, LAT:] = latent[:, LAT:]
+
+    pl.semaphore_wait(barrier, 6)
+
+    def x_step1(plane, s):
+        ref = keys_ref.at[planes[plane] + x, core, sets[s]]
+        for d in range(2):
+            i = (plane * 2 + s) * 2 + d
+            go(ref, x1send.at[i], x1got.at[i], to_x[d])
+
+    for s in range(2):
+        ref = keys_ref.at[mine, core, sets[s]]
+        go(ref, zsend.at[s], zgot.at[s], to_z)
+        x_step1(0, s)
+    for s, part_rows in enumerate((pl.ds(direct, rows - direct), pl.ds(0, direct))):
+        i = s * 4
+        go(keys_ref.at[mine, core, part_rows], csend.at[i], cgot.at[i], to_core)
+
+    for h in range(q_ref.shape[0]):
+        q = q_ref[h]
+        lat = jnp.dot(q[:, :NOPE], uk_ref[h], preferred_element_type=jnp.float32)
+        qf_ref[h, :, :LAT] = lat.astype(jnp.bfloat16)
+        qf_ref[h, :, LAT:] = q[:, NOPE:]
+
+    def x_step2(plane, s):
+        for d, source in enumerate((x_down, x_up)):
+            i = (plane * 2 + s) * 2 + d
+            got(keys_ref.at[planes[plane] + source, core, sets[s]], x1send.at[i], x1got.at[i])
+            ref = keys_ref.at[planes[plane] + source, core, set_halves[s][d]]
+            go(ref, x2send.at[i], x2got.at[i], to_x[d])
+
+    def x_finish(plane, s):
+        for d in range(2):
+            i = (plane * 2 + s) * 2 + d
+            ref = keys_ref.at[planes[plane] + x_far, core, set_halves[s][d]]
+            got(ref, x2send.at[i], x2got.at[i])
+
+    around = (x, x_up, x_far, x_down)
+
+    def block(plane, r):
+        return planes[plane] + around[r]
+
+    onward = {(0, 1): 0, (0, 2): 0, (0, 3): 1, (1, 0): 1, (1, 1): 0, (1, 2): 0, (1, 3): 1}
+    order = {0: (1, 3, 2), 1: (0, 1, 3, 2)}
+
+    def y_step1(plane, rs):
+        for r in rs:
+            ref = keys_ref.at[block(plane, r), core, strip(y)]
+            for d in range(2):
+                i = (plane * 2 + d) * 4 + r
+                go(ref, y1send.at[i], y1got.at[i], to_y[d])
+
+    def y_step2(plane):
+        for r in order[plane]:
+            for d, source in enumerate((y_down, y_up)):
+                i = (plane * 2 + d) * 4 + r
+                ref = keys_ref.at[block(plane, r), core, strip(source)]
+                got(ref, y1send.at[i], y1got.at[i])
+                if onward[(plane, r)] == d:
+                    i = plane * 4 + r
+                    go(ref, y2send.at[i], y2got.at[i], to_y[d])
+
+    halves = (pl.ds(direct, rows - direct), pl.ds(0, direct))
+
+    def to_sibling(plane, s, r):
+        i = (plane * 2 + s) * 4 + r
+        ref = keys_ref.at[block(plane, r), core, halves[s]]
+        go(ref, csend.at[i], cgot.at[i], to_core)
+
+    def y_finish(plane):
+        for r in order[plane]:
+            i = plane * 4 + r
+            ref = keys_ref.at[block(plane, r), core, strip(y_far)]
+            got(ref, y2send.at[i], y2got.at[i])
+            to_sibling(plane, 0, r)
+
+    got(keys_ref.at[block(1, 0), core, sets[0]], zsend.at[0], zgot.at[0])
+    x_step1(1, 0)
+    x_step2(0, 0)
+    y_step1(0, (1, 3))
+    y_step1(1, (0,))
+    got(keys_ref.at[block(1, 0), core, sets[1]], zsend.at[1], zgot.at[1])
+    x_step1(1, 1)
+    to_sibling(1, 1, 0)
+    x_step2(1, 0)
+    y_step1(1, (1, 3))
+    x_finish(0, 0)
+    y_step1(0, (2,))
+    x_step2(0, 1)
+    to_sibling(0, 1, 1)
+    to_sibling(0, 1, 3)
+    x_finish(1, 0)
+    y_step1(1, (2,))
+    y_step2(0)
+    x_step2(1, 1)
+    to_sibling(1, 1, 1)
+    to_sibling(1, 1, 3)
+    x_finish(0, 1)
+    to_sibling(0, 1, 2)
+    y_step2(1)
+    y_finish(0)
+    x_finish(1, 1)
+    to_sibling(1, 1, 2)
+    y_finish(1)
+    for plane in range(2):
+        for s in range(2):
+            for r in range(4):
+                i = (plane * 2 + s) * 4 + r
+                ref = keys_ref.at[block(plane, r), 1 - core, halves[s]]
+                got(ref, csend.at[i], cgot.at[i])
+    for one in pending:
+        one.wait_send()
+
+
+def gather(by_head, latents, scale_row, w_uk):
+    heads, rows, _ = by_head.shape
+    width = latents.shape[1]
+    dma = pltpu.SemaphoreType.DMA
+    vmem = pl.BlockSpec(memory_space=pltpu.VMEM)
+    counts = (2, 8, 8, 16, 8, 16)
+    return pl.pallas_call(
+        gather_kernel,
+        out_shape=(
+            jax.ShapeDtypeStruct((8, 2, rows, width), jnp.bfloat16),
+            jax.ShapeDtypeStruct((heads, rows, width), jnp.bfloat16),
+        ),
+        in_specs=[vmem] * 4,
+        out_specs=(vmem, vmem),
+        scratch_shapes=[dma((n,)) for n in counts for _ in range(2)],
+        compiler_params=pltpu.CompilerParams(
+            collective_id=1, has_side_effects=True, vmem_limit_bytes=20 << 20
+        ),
+        name="gather",
+    )(by_head, latents, scale_row, w_uk)
+
+
 def shards(query, latents, lat_scale, doc_lengths, w_uk, w_uv, w_o):
-    ctx_index = lax.axis_index("ctx").astype(jnp.int32).reshape(1)
-    scaled = (latents[:, :LAT].astype(jnp.float32) * lat_scale[:, None]).astype(jnp.bfloat16)
-    deq = jnp.concatenate([scaled, latents[:, LAT:]], axis=1)
-    deq = lax.all_gather(deq, "ctx", axis=0, tiled=True)
     by_head = jnp.transpose(query, (1, 0, 2))
-    head_out = attention(doc_lengths, ctx_index, by_head, w_uk, deq, w_uv)
+    keys, query_full = gather(by_head, latents, lat_scale.reshape(1, -1), w_uk)
+    width = latents.shape[1]
+    head_out = attention(
+        doc_lengths, query_full.reshape(-1, width), keys.reshape(-1, width), w_uv
+    )
     return project_and_reduce(head_out, w_o)
 
 

time: 150 us -> 86.5 us (0.58)
  waiting for transfers between devices: 57.7 us -> 0 us
  Pallas kernels: 65.2 us -> 78.8 us
  between operations: 13.4 us -> 0.06 us
  local copies, waits for them, and re-layouts: 9.78 us -> 6 us
  other arithmetic: 1.54 us -> 0 us
    all_gather x1 -> x0, waiting for transfers between devices: 57.7 us -> none  [shards(): deq = lax.all_gather(deq, 'ctx', axis=0, tiled=True)]
    pallas_call x0 -> x1, Pallas kernels: none -> 24.7 us  [gather(): pl.pallas_call(gather_kernel, out_shape=(jax.ShapeDtypeStruct((8, 2, rows...]
    pallas_call x1, Pallas kernels: 34.6 us -> 24.9 us  [attention(): pl.pallas_call(attention_kernel, out_shape=jax.ShapeDtypeStruct((TOK, hea...]
    unnamed x12 -> x11, local copies, waits for them, and re-layouts: 8.05 us -> 6 us
    slice x2 -> x0, local copies, waits for them, and re-layouts: 1.73 us -> none  [the longest x1 0.97 us: shards(): latents[:, :LAT].astype(jnp.float32) * lat_scale[:, None]]
  transfers between devices with their start and end apart: 1 -> 0, of which waited for: 1 -> 0; matrix products, arithmetic and copies ran while one was open for 1% -> 0% of each run, Pallas kernels for 0% -> 0%
where the time goes in v3:
time: 86.5 us; the launch traced here: 84.9 us
  Pallas kernels  78.8 us (91%)
  local copies, waits for them, and re-layouts  6 us (7%)
    pallas_call x1, Pallas kernels, project_and_reduce(): pl.pallas_call(reduce_kernel, out_shape=jax.ShapeDtypeStruct((rows, cols)...  29.2 us
    pallas_call x1, Pallas kernels, attention(): pl.pallas_call(attention_kernel, out_shape=jax.ShapeDtypeStruct((TOK, hea...  24.9 us
    pallas_call x1, Pallas kernels, gather(): pl.pallas_call(gather_kernel, out_shape=(jax.ShapeDtypeStruct((8, 2, rows...  24.7 us
    unnamed x11, local copies, waits for them, and re-layouts  6 us

profile of v3, /device:TPU:67, one launch (start us, length us, event | category | flops | bytes accessed | tf_op | source)
XLA Modules:
  0.0 84.9 jit_solution(15663818942632613488)
XLA Ops:
  0.0 0.0 copy-start
  0.0 1.2 %copy.9.latents_ref = bf16[256,576]{1,0:T(8,128)(2,1)S(1)} copy(bf16[256,576]{0,1:T(8,128)(2,1)} %param.8) | data formatting | bytes 589824 | tf_op args[1]
  1.3 1.4 %copy.8 = bf16[256,8,192]{2,0,1:T(8,128)(2,1)S(1)} copy(bf16[256,8,192]{0,2,1:T(8,128)(2,1)} %param.7) | data formatting | bytes 1572864 | tf_op args[0]
  2.7 0.0 copy-start.1
  2.7 1.2 %copy-done.1 = bf16[8,128,512]{2,1,0:T(8,128)(2,1)S(1)} copy-done((bf16[8,128,512]{2,1,0:T(8,128)(2,1)S(1)}, bf16[8,128,512]{2,1,0:T(8,128)(2,1)}, u32[]{:S(2)}) %copy-start.1) | copy-done | bytes 1048600
  3.9 0.0 copy-start.2
  3.9 0.7 copy-done.2
  4.6 24.7 %gather.1 = (bf16[8,2,256,576]{3,2,1,0:T(8,128)(2,1)S(1)}, bf16[8,256,576]{2,1,0:T(8,128)(2,1)S(1)}) custom-call(bf16[8,256,192]{2,1,0:T(8,128)(2,1)S(1)} %bitcast.5, bf16[256,576]{1,0:T(8,128)(2,1)S(1)} %copy.9.latents_ref, f32[1,256]{1,0:T(1,128)S(1)} %bitcast.7, bf16[8,128,512]{2,1,0:T(8,128)(2,1)S(1)} %copy-done.1), custom_call_target="tpu_custom_call" | custom-call | tf_op jit(solution)/shard_map/gather/pallas_call | solution.py:493
  29.3 0.0 copy-done
  29.3 0.0 copy-start.3
  29.3 0.6 copy-done.3
  30.0 24.9 %attention.1.x_ref = bf16[256,1024]{1,0:T(8,128)(2,1)S(1)} custom-call(s32[8]{0:T(128)S(1)} %copy-done.3, bf16[2048,576]{1,0:T(8,128)(2,1)S(1)} %bitcast.6, bf16[4096,576]{1,0:T(8,128)(2,1)S(1)} %bitcast.4, bf16[8,512,128]{2,1,0:T(8,128)(2,1)S(1)} %copy-done), custom_call_target="tpu_custom_call" | custom-call | tf_op jit(solution)/shard_map/attention/pallas_call | solution.py:123
  54.9 29.2 %project_and_reduce.1 = bf16[256,896]{1,0:T(8,128)(2,1)S(1)} custom-call(bf16[256,1024]{1,0:T(8,128)(2,1)S(1)} %attention.1.x_ref, bf16[1024,7168]{1,0:T(8,128)(2,1)} %w_ref.1), custom_call_target="tpu_custom_call" | custom-call | tf_op jit(solution)/shard_map/project_and_reduce/pallas_call | solution.py:277
  84.1 0.8 copy.11
Async XLA Ops:
  0.0 29.3 %copy-start = (bf16[8,512,128]{2,1,0:T(8,128)(2,1)S(1)}, bf16[8,512,128]{2,1,0:T(8,128)(2,1)}, u32[]{:S(2)}) copy-start(bf16[8,512,128]{2,1,0:T(8,128)(2,1)} %uv_ref.1) | copy-start | bytes 3145732
  2.7 1.2 %copy-start.1 = (bf16[8,128,512]{2,1,0:T(8,128)(2,1)S(1)}, bf16[8,128,512]{2,1,0:T(8,128)(2,1)}, u32[]{:S(2)}) copy-start(bf16[8,128,512]{2,1,0:T(8,128)(2,1)} %uk_ref.1) | copy-start | bytes 3145732
  3.9 0.7 copy-start.2
  29.3 0.7 copy-start.3

commit v4 on v2

v4 whole, which is shorter than its diff:
```python
import jax
import jax.numpy as jnp
from jax import lax
from jax.experimental import pallas as pl
from jax.experimental.pallas import tpu as pltpu
from jax.sharding import PartitionSpec as P

LAT = 512
NOPE = 128
QDIM = 192
VDIM = 128
GROUP = 4
NEG = -1e30
MESH = pl.DeviceIdType.MESH
EXP_SCALE = float(QDIM) ** -0.5 * 1.4426950408889634


def attend_kernel(
    lens_hbm, q_hbm, latents_hbm, scale_hbm, uk_hbm, uv_hbm, out_ref,
    lens_ref, q_ref, latents_ref, scale_ref, uk_ref, uv_ref,
    keys_ref, qf_ref, s_ref, m_ref, l_ref, acc_ref, first_ref, load_sem,
    zsend, zgot, x1send, x1got, x2send, x2got, csend, cgot,
):
    rows = latents_ref.shape[1]
    heads = q_ref.shape[0]
    block_rows = GROUP * rows
    groups = heads // GROUP
    ctx = lax.axis_index("ctx")
    head = lax.axis_index("head")
    core = lax.rem(ctx, 2)
    x = lax.rem(ctx // 2, 4)
    hi = ctx // 8
    y = lax.rem(head, 4)
    lo = head // 4
    x_up, x_down, x_far = lax.rem(x + 1, 4), lax.rem(x + 3, 4), lax.rem(x + 2, 4)
    planes = (hi * 4, (1 - hi) * 4)
    around = (x, x_up, x_far, x_down)

    loads = [
        pltpu.make_async_copy(src, dst, load_sem.at[i])
        for i, (src, dst) in enumerate(
            (
                (latents_hbm, latents_ref),
                (scale_hbm, scale_ref),
                (uk_hbm, uk_ref),
                (lens_hbm, lens_ref),
                (uv_hbm, uv_ref),
                (q_hbm, q_ref),
            )
        )
    ]
    for load in loads:
        load.start()

    def place(a, b, c, d, e):
        return {"ctx": a * 8 + b * 2 + c, "head": d * 4 + e}

    to_x = (place(hi, x_up, core, lo, y), place(hi, x_down, core, lo, y))
    to_z = place(1 - hi, x, core, 1 - lo, y)
    to_core = place(hi, x, 1 - core, lo, y)

    def copy(src, dst, ssem, rsem, target):
        return pltpu.make_async_remote_copy(
            src_ref=src, dst_ref=dst, send_sem=ssem, recv_sem=rsem,
            device_id=target, device_id_type=MESH,
        )

    pending = []

    def go(ref, ssem, rsem, target):
        one = copy(ref, ref, ssem, rsem, target)
        one.start()
        pending.append(one)

    def got(ref, ssem, rsem):
        copy(ref, ref, ssem, rsem, to_core).wait_recv()

    barrier = pltpu.get_barrier_semaphore()
    for target in (*to_x, to_z, to_core):
        pl.semaphore_signal(barrier, inc=1, device_id=target, device_id_type=MESH)

    def block(plane, r):
        return planes[plane] + around[r]

    loads[0].wait()
    loads[1].wait()
    mine = block(0, 0)
    latent = latents_ref[...].astype(jnp.float32)
    keys_ref[mine, core, :, :LAT] = (latent[:LAT] * scale_ref[...]).T.astype(jnp.bfloat16)
    keys_ref[mine, core, :, LAT:] = latent[LAT:].T.astype(jnp.bfloat16)

    pl.semaphore_wait(barrier, 4)

    parts = (pl.ds(0, rows // 2), pl.ds(rows // 2, rows // 2))

    def x_step1(plane):
        for d in range(2):
            i = plane * 2 + d
            go(keys_ref.at[block(plane, 0), core], x1send.at[i], x1got.at[i], to_x[d])

    def to_sibling(plane, r):
        i = plane * 4 + r
        go(keys_ref.at[block(plane, r), core], csend.at[i], cgot.at[i], to_core)

    def from_sibling(plane, r):
        i = plane * 4 + r
        got(keys_ref.at[block(plane, r), 1 - core], csend.at[i], cgot.at[i])

    def x_step2(plane):
        for d, r in enumerate((3, 1)):
            i = plane * 2 + d
            got(keys_ref.at[block(plane, r), core], x1send.at[i], x1got.at[i])
            go(keys_ref.at[block(plane, r), core, parts[d]], x2send.at[i], x2got.at[i], to_x[d])
        to_sibling(plane, 1)
        to_sibling(plane, 3)

    def x_finish(plane):
        for d in range(2):
            i = plane * 2 + d
            got(keys_ref.at[block(plane, 2), core, parts[d]], x2send.at[i], x2got.at[i])
        to_sibling(plane, 2)

    def from_z():
        got(keys_ref.at[block(1, 0), core], zsend.at[0], zgot.at[0])
        x_step1(1)
        to_sibling(1, 0)

    go(keys_ref.at[mine, core], zsend.at[0], zgot.at[0], to_z)
    x_step1(0)
    to_sibling(0, 0)

    loads[2].wait()
    loads[5].wait()
    for h in range(heads):
        q = q_ref[h].astype(jnp.float32).T.astype(jnp.bfloat16)
        lat = jnp.dot(q[:, :NOPE], uk_ref[h], preferred_element_type=jnp.float32)
        qf_ref[h, :, :LAT] = lat.astype(jnp.bfloat16)
        qf_ref[h, :, LAT:] = q[:, NOPE:]

    loads[3].wait()
    t0 = ctx * rows
    qpos = t0 + lax.broadcasted_iota(jnp.int32, (rows, 128), 0)
    first = jnp.zeros_like(qpos)
    end = jnp.int32(0)
    for k in range(lens_ref.shape[0]):
        end = end + lens_ref[k]
        first = jnp.where(qpos >= end, end, first)
    first_ref[...] = jnp.concatenate([first] * GROUP, axis=0)
    m_ref[...] = jnp.full_like(m_ref, NEG)

    def scores(p, k, diagonal):
        j = p * 2 + k
        kpos = j * rows + lax.broadcasted_iota(jnp.int32, (1, 128), 1)

        def one_group(g, carry):
            q = qf_ref[pl.ds(g * GROUP, GROUP)].reshape(block_rows, -1)
            s = lax.dot_general(
                q, keys_ref[p, k], (((1,), (1,)), ((), ())), preferred_element_type=jnp.float32
            )
            here = pl.ds(pl.multiple_of(g * block_rows, block_rows), block_rows)
            top = m_ref[here]
            for lane in range(0, rows, 128):
                allowed = first_ref[...] <= kpos + lane
                if diagonal:
                    local = lax.broadcasted_iota(jnp.int32, (block_rows, 128), 0)
                    ahead = lane + lax.broadcasted_iota(jnp.int32, (block_rows, 128), 1)
                    allowed = allowed & (ahead <= lax.rem(local, rows))
                part = jnp.where(allowed, s[:, lane : lane + 128], NEG)
                s_ref[j, here, lane : lane + 128] = part
                top = jnp.maximum(top, part)
            m_ref[here] = top
            return carry

        lax.fori_loop(0, groups, one_group, 0)

    def tiles(plane, r, count, k):
        def one(i, carry):
            p = planes[plane] + lax.rem(x + r + 2 * i, 4)

            @pl.when(p * 2 + k < ctx)
            def _():
                scores(p, k, False)

            return carry

        lax.fori_loop(0, count, one, 0)

    scores(mine, core, True)
    from_z()
    x_step2(0)
    from_sibling(0, 0)
    tiles(0, 0, 1, 1 - core)
    tiles(0, 1, 2, core)
    x_step2(1)
    x_finish(0)
    tiles(1, 0, 1, core)
    for r in (1, 3):
        from_sibling(0, r)
    from_sibling(1, 0)
    tiles(0, 1, 2, 1 - core)
    tiles(1, 0, 1, 1 - core)
    x_finish(1)
    tiles(1, 1, 2, core)
    tiles(0, 2, 1, core)
    for r in (1, 3):
        from_sibling(1, r)
    tiles(1, 1, 2, 1 - core)
    tiles(1, 2, 1, core)
    from_sibling(0, 2)
    from_sibling(1, 2)
    tiles(0, 2, 1, 1 - core)
    tiles(1, 2, 1, 1 - core)

    @pl.when(core == 0)
    def _():
        s_ref[ctx + 1] = jnp.full(s_ref.shape[1:], NEG, jnp.float32)

    loads[4].wait()

    def context_of(g, carry):
        here = pl.ds(pl.multiple_of(g * block_rows, block_rows), block_rows)
        m = jnp.max(m_ref[here], axis=1, keepdims=True)
        m_ref[here] = jnp.broadcast_to(m, (block_rows, 128))
        l_ref[...] = jnp.zeros_like(l_ref)
        acc_ref[...] = jnp.zeros_like(acc_ref)

        def weigh(p, carry):
            top = m_ref[here]
            weights = []
            total = l_ref[...]
            for k in range(2):
                for lane in range(0, rows, 128):
                    s = s_ref[2 * p + k, here, lane : lane + 128]
                    w = jnp.exp2((s - top) * EXP_SCALE)
                    total = total + w
                    weights.append(w.astype(jnp.bfloat16))
            l_ref[...] = total
            values = keys_ref[p, :, :, :LAT].reshape(2 * rows, LAT)
            acc_ref[...] += jnp.dot(
                jnp.concatenate(weights, axis=1), values, preferred_element_type=jnp.float32
            )
            return carry

        lax.fori_loop(0, ctx // 2 + 1, weigh, 0)
        inverse = 1.0 / jnp.sum(l_ref[...], axis=1, keepdims=True)
        context = (acc_ref[...] * inverse).astype(jnp.bfloat16)
        for i in range(GROUP):
            h = g * GROUP + i
            one = jnp.dot(
                context[i * rows : (i + 1) * rows], uv_ref[h], preferred_element_type=jnp.float32
            )
            out_ref[:, pl.ds(pl.multiple_of(h * VDIM, VDIM), VDIM)] = one.astype(jnp.bfloat16)
        return carry

    lax.fori_loop(0, groups, context_of, 0)
    for one in pending:
        one.wait_send()


def attend(doc_lengths, by_head, latents, scale_row, w_uk, w_uv):
    heads, _, rows = by_head.shape
    width = latents.shape[0]
    dma = pltpu.SemaphoreType.DMA
    vmem = pltpu.VMEM
    outside = pl.BlockSpec(memory_space=pl.ANY)
    whole = pl.BlockSpec(memory_space=pltpu.VMEM)
    block_rows = GROUP * rows
    return pl.pallas_call(
        attend_kernel,
        out_shape=jax.ShapeDtypeStruct((rows, heads * VDIM), jnp.bfloat16),
        in_specs=[outside] * 6,
        out_specs=whole,
        scratch_shapes=[
            pltpu.SMEM(doc_lengths.shape, jnp.int32),
            vmem(by_head.shape, by_head.dtype),
            vmem(latents.shape, latents.dtype),
            vmem(scale_row.shape, scale_row.dtype),
            vmem(w_uk.shape, w_uk.dtype),
            vmem(w_uv.shape, w_uv.dtype),
            vmem((8, 2, rows, width), jnp.bfloat16),
            vmem((heads, rows, width), jnp.bfloat16),
            vmem((16, heads * rows, rows), jnp.float32),
            vmem((heads * rows, 128), jnp.float32),
            vmem((block_rows, 128), jnp.float32),
            vmem((block_rows, LAT), jnp.float32),
            vmem((block_rows, 128), jnp.int32),
            dma((6,)),
            dma((1,)), dma((1,)),
            dma((4,)), dma((4,)),
            dma((4,)), dma((4,)),
            dma((8,)), dma((8,)),
        ],
        compiler_params=pltpu.CompilerParams(
            collective_id=1, has_side_effects=True, vmem_limit_bytes=61 << 20
        ),
        name="attend",
    )(doc_lengths, by_head, latents, scale_row, w_uk, w_uv)


def reduce_kernel(
    x_hbm, w_ref, out_ref, x_ref, x_sem, wbuf, own, zrecv, y1recv, y2recv, ysecond1, ysecond2, zlast,
    wsem, zsend, zgot, y1send, y1got, y2send, y2got, s1send, s1got, s2send, s2got, lsend, lgot,
):
    cols = out_ref.shape[1]
    half = out_ref.shape[0] // 2
    quarter = half // 2
    me = lax.axis_index("head")
    y = lax.rem(me, 4)
    z = me // 4
    up = z * 4 + lax.rem(y + 1, 4)
    down = z * 4 + lax.rem(y + 3, 4)
    across = (1 - z) * 4 + y
    blocks = ((2, 0), (2, 1), (1, 0), (3, 0), (1, 1), (3, 1), (0, 0), (0, 1))
    slot = {key: k for k, key in enumerate(blocks)}
    first = pl.ds(0, half)
    second = pl.ds(half, half)

    def fetch(k):
        shift, mine = blocks[k]
        plane = z if mine else 1 - z
        start = pl.multiple_of((plane * 4 + lax.rem(y + shift, 4)) * cols, 128)
        return pltpu.make_async_copy(w_ref.at[:, pl.ds(start, cols)], wbuf.at[k], wsem.at[k])

    def send(src, dst, ssem, rsem, target):
        return pltpu.make_async_remote_copy(
            src_ref=src, dst_ref=dst, send_sem=ssem, recv_sem=rsem,
            device_id={"head": target}, device_id_type=MESH,
        )

    load = pltpu.make_async_copy(x_hbm, x_ref, x_sem.at[0])
    load.start()
    for k in range(8):
        fetch(k).start()
    barrier = pltpu.get_barrier_semaphore()
    for target in (up, down, across):
        pl.semaphore_signal(barrier, inc=1, device_id={"head": target}, device_id_type=MESH)
    load.wait()
    pl.semaphore_wait(barrier, 3)

    pending = []

    def go(copy):
        copy.start()
        pending.append(copy)

    def across_copy(i, k):
        return send(own.at[k, first], zrecv.at[i], zsend.at[i], zgot.at[i], across)

    def step1(k, base, buf, ssem, rsem, i):
        go(send(own.at[k, pl.ds(base, quarter)], buf.at[i], ssem.at[i], rsem.at[i], up))
        go(
            send(
                own.at[k, pl.ds(base + quarter, quarter)],
                buf.at[i + 1], ssem.at[i + 1], rsem.at[i + 1], down,
            )
        )

    across_order = (2, 1, 3, 0)
    across_copies = {}

    def compute(k):
        fetch(k).wait()
        own[k] = jnp.dot(x_ref[...], wbuf[k], preferred_element_type=jnp.float32).astype(
            jnp.bfloat16
        )
        shift, mine = blocks[k]
        if not mine:
            i = across_order.index(shift)
            across_copies[i] = across_copy(i, k)
            go(across_copies[i])
        if shift == 2:
            step1(k, half, y1recv, y1send, y1got, 2 * mine)

    def add_rows(k, rows, *terms):
        total = own[k, rows].astype(jnp.float32)
        for term in terms:
            total = total + term.astype(jnp.float32)
        return total

    copies = {}

    def y_first_step2(mine):
        for side, (shift, target, offset) in enumerate(((1, up, 0), (3, down, quarter))):
            k = slot[(shift, mine)]
            i = 2 * mine + side
            rows = pl.ds(half + offset, quarter)
            send(
                own.at[0, pl.ds(0, quarter)], y1recv.at[i], y1send.at[i], y1got.at[i], target
            ).wait_recv()
            own[k, rows] = add_rows(k, rows, y1recv[i]).astype(jnp.bfloat16)
            go(send(own.at[k, second], y2recv.at[i], y2send.at[i], y2got.at[i], target))

    def got(buf, i, ssem, rsem, rows):
        send(own.at[0, pl.ds(0, rows)], buf.at[i], ssem.at[i], rsem.at[i], across).wait_recv()

    for k in range(6):
        compute(k)
    y_first_step2(0)
    for k in range(6, 8):
        compute(k)
    y_first_step2(1)

    got(zrecv, 0, zsend, zgot, half)
    k = slot[(2, 1)]
    own[k, first] = add_rows(k, first, zrecv[0]).astype(jnp.bfloat16)
    step1(k, 0, ysecond1, s1send, s1got, 0)

    got(y2recv, 0, y2send, y2got, half)
    got(y2recv, 1, y2send, y2got, half)
    k = slot[(0, 0)]
    own[k, second] = add_rows(k, second, y2recv[0], y2recv[1]).astype(jnp.bfloat16)
    go(send(own.at[k, second], zlast.at[0], lsend.at[0], lgot.at[0], across))

    for side, (shift, target, offset) in enumerate(((1, up, 0), (3, down, quarter))):
        k = slot[(shift, 1)]
        got(zrecv, 1 + side, zsend, zgot, half)
        got(ysecond1, side, s1send, s1got, quarter)
        own[k, first] = add_rows(k, first, zrecv[1 + side]).astype(jnp.bfloat16)
        rows = pl.ds(offset, quarter)
        own[k, rows] = add_rows(k, rows, ysecond1[side]).astype(jnp.bfloat16)
        go(send(own.at[k, first], ysecond2.at[side], s2send.at[side], s2got.at[side], target))

    k = slot[(0, 1)]
    got(y2recv, 2, y2send, y2got, half)
    got(y2recv, 3, y2send, y2got, half)
    got(zlast, 0, lsend, lgot, half)
    out_ref[second] = add_rows(k, second, y2recv[2], y2recv[3], zlast[0]).astype(jnp.bfloat16)
    got(zrecv, 3, zsend, zgot, half)
    got(ysecond2, 0, s2send, s2got, half)
    got(ysecond2, 1, s2send, s2got, half)
    out_ref[first] = add_rows(k, first, zrecv[3], ysecond2[0], ysecond2[1]).astype(jnp.bfloat16)
    for copy in pending:
        copy.wait_send()


def project_and_reduce(head_out, w_o):
    rows, inner = head_out.shape
    cols = w_o.shape[1] // 8
    half = rows // 2
    dma = pltpu.SemaphoreType.DMA
    return pl.pallas_call(
        reduce_kernel,
        out_shape=jax.ShapeDtypeStruct((rows, cols), jnp.bfloat16),
        in_specs=[pl.BlockSpec(memory_space=pl.ANY)] * 2,
        out_specs=pl.BlockSpec(memory_space=pltpu.VMEM),
        scratch_shapes=[
            pltpu.VMEM((rows, inner), jnp.bfloat16),
            dma((1,)),
            pltpu.VMEM((8, inner, cols), jnp.bfloat16),
            pltpu.VMEM((8, rows, cols), jnp.bfloat16),
            pltpu.VMEM((4, half, cols), jnp.bfloat16),
            pltpu.VMEM((4, half // 2, cols), jnp.bfloat16),
            pltpu.VMEM((4, half, cols), jnp.bfloat16),
            pltpu.VMEM((2, half // 2, cols), jnp.bfloat16),
            pltpu.VMEM((2, half, cols), jnp.bfloat16),
            pltpu.VMEM((1, half, cols), jnp.bfloat16),
            dma((8,)),
            dma((4,)), dma((4,)),
            dma((4,)), dma((4,)),
            dma((4,)), dma((4,)),
            dma((2,)), dma((2,)),
            dma((2,)), dma((2,)),
            dma((1,)), dma((1,)),
        ],
        compiler_params=pltpu.CompilerParams(
            collective_id=0, has_side_effects=True, vmem_limit_bytes=40 << 20
        ),
        name="project_and_reduce",
    )(head_out, w_o)


def shards(query, latents, lat_scale, doc_lengths, w_uk, w_uv, w_o):
    by_head = jnp.transpose(query, (1, 2, 0))
    head_out = attend(doc_lengths, by_head, latents.T, lat_scale.reshape(1, -1), w_uk, w_uv)
    return project_and_reduce(head_out, w_o)


def solution(mesh):
    placed = (
        P("ctx", "head", None),
        P("ctx", None),
        P("ctx"),
        P(),
        P("head", None, None),
        P("head", None, None),
        P("head", None),
    )
    return jax.shard_map(
        shards, mesh=mesh, in_specs=placed, out_specs=P("ctx", "head"), check_vma=False
    )
```

time: 150 us -> 84.1 us (0.56)
  the two profiles are of different devices: /device:TPU:67 before, /device:TPU:70 now
where the time goes in v4:
time: 84.1 us; the launch traced here: 83.3 us
  Pallas kernels  81.5 us (97%)
  local copies, waits for them, and re-layouts  1.8 us (2%)
    pallas_call x1, Pallas kernels, attend(): pl.pallas_call(attend_kernel, out_shape=jax.ShapeDtypeStruct((rows, heads...  52.5 us
    pallas_call x1, Pallas kernels, project_and_reduce(): pl.pallas_call(reduce_kernel, out_shape=jax.ShapeDtypeStruct((rows, cols)...  29 us
    unnamed x3, local copies, waits for them, and re-layouts  1.8 us

profile of v4, /device:TPU:70, one launch (start us, length us, event | category | flops | bytes accessed | tf_op | source)
XLA Modules:
  0.0 83.3 jit_solution(17565388405781832444)
XLA Ops:
  0.0 52.5 %attend.1.x_hbm = bf16[256,1024]{1,0:T(8,128)(2,1)} custom-call(s32[8]{0:T(128)} %lens_hbm.1, bf16[8,192,256]{2,1,0:T(8,128)(2,1)} %bitcast.3, bf16[576,256]{1,0:T(8,128)(2,1)} %bitcast.4, f32[1,256]{1,0:T(1,128)} %bitcast.5, bf16[8,128,512]{2,1,0:T(8,128)(2,1)} %uk_hbm.1, bf16[8,512,128]{2,1,0:T(8,128)(2,1)} %uv_hbm.1), custom_call_target="tpu_custom_call" | custom-call | tf_op jit(solution)/shard_map/attend/pallas_call | solution.py:268
  52.5 0.0 copy-start
  52.5 1.0 %copy-done = bf16[256,1024]{1,0:T(8,128)(2,1)S(1)} copy-done((bf16[256,1024]{1,0:T(8,128)(2,1)S(1)}, bf16[256,1024]{1,0:T(8,128)(2,1)}, u32[]{:S(2)}) %copy-start) | copy-done | bytes 524312
  53.5 29.0 %project_and_reduce.1 = bf16[256,896]{1,0:T(8,128)(2,1)S(1)} custom-call(bf16[256,1024]{1,0:T(8,128)(2,1)S(1)} %copy-done, bf16[1024,7168]{1,0:T(8,128)(2,1)} %w_ref.1), custom_call_target="tpu_custom_call" | custom-call | tf_op jit(solution)/shard_map/project_and_reduce/pallas_call | solution.py:441
  82.6 0.8 copy.9
Async XLA Ops:
  52.5 1.0 %copy-start = (bf16[256,1024]{1,0:T(8,128)(2,1)S(1)}, bf16[256,1024]{1,0:T(8,128)(2,1)}, u32[]{:S(2)}) copy-start(bf16[256,1024]{1,0:T(8,128)(2,1)} %attend.1.x_hbm) | copy-start | bytes 1572868

commit v5 on v4

--- a/solution.py
+++ b/solution.py
@@ -19,7 +19,8 @@
     lens_hbm, q_hbm, latents_hbm, scale_hbm, uk_hbm, uv_hbm, out_ref,
     lens_ref, q_ref, latents_ref, scale_ref, uk_ref, uv_ref,
     keys_ref, qf_ref, s_ref, m_ref, l_ref, acc_ref, first_ref, load_sem,
-    zsend, zgot, x1send, x1got, x2send, x2got, csend, cgot,
+    zsend, zgot, x1send, x1got, x2send, x2got, s1send, s1got, s2send, s2got,
+    y1send, y1got, y2send, y2got, csend, cgot,
 ):
     rows = latents_ref.shape[1]
     heads = q_ref.shape[0]
@@ -33,6 +34,7 @@
     y = lax.rem(head, 4)
     lo = head // 4
     x_up, x_down, x_far = lax.rem(x + 1, 4), lax.rem(x + 3, 4), lax.rem(x + 2, 4)
+    y_up, y_down, y_far = lax.rem(y + 1, 4), lax.rem(y + 3, 4), lax.rem(y + 2, 4)
     planes = (hi * 4, (1 - hi) * 4)
     around = (x, x_up, x_far, x_down)
 
@@ -56,6 +58,7 @@
         return {"ctx": a * 8 + b * 2 + c, "head": d * 4 + e}
 
     to_x = (place(hi, x_up, core, lo, y), place(hi, x_down, core, lo, y))
+    to_y = (place(hi, x, core, lo, y_up), place(hi, x, core, lo, y_down))
     to_z = place(1 - hi, x, core, 1 - lo, y)
     to_core = place(hi, x, 1 - core, lo, y)
 
@@ -76,7 +79,7 @@
         copy(ref, ref, ssem, rsem, to_core).wait_recv()
 
     barrier = pltpu.get_barrier_semaphore()
-    for target in (*to_x, to_z, to_core):
+    for target in (*to_x, *to_y, to_z, to_core):
         pl.semaphore_signal(barrier, inc=1, device_id=target, device_id_type=MESH)
 
     def block(plane, r):
@@ -89,14 +92,19 @@
     keys_ref[mine, core, :, :LAT] = (latent[:LAT] * scale_ref[...]).T.astype(jnp.bfloat16)
     keys_ref[mine, core, :, LAT:] = latent[LAT:].T.astype(jnp.bfloat16)
 
-    pl.semaphore_wait(barrier, 4)
+    pl.semaphore_wait(barrier, 6)
 
     parts = (pl.ds(0, rows // 2), pl.ds(rows // 2, rows // 2))
-
-    def x_step1(plane):
-        for d in range(2):
-            i = plane * 2 + d
-            go(keys_ref.at[block(plane, 0), core], x1send.at[i], x1got.at[i], to_x[d])
+    width = rows // 4
+
+    def strip(index):
+        return pl.ds(pl.multiple_of(index * width, 16), width)
+
+    def strip_half(index, which):
+        return pl.ds(pl.multiple_of(index * width + which * (width // 2), 16), width // 2)
+
+    def at(plane, r, part):
+        return keys_ref.at[block(plane, r), core, part]
 
     def to_sibling(plane, r):
         i = plane * 4 + r
@@ -106,36 +114,83 @@
         i = plane * 4 + r
         got(keys_ref.at[block(plane, r), 1 - core], csend.at[i], cgot.at[i])
 
-    def x_step2(plane):
-        for d, r in enumerate((3, 1)):
-            i = plane * 2 + d
-            got(keys_ref.at[block(plane, r), core], x1send.at[i], x1got.at[i])
-            go(keys_ref.at[block(plane, r), core, parts[d]], x2send.at[i], x2got.at[i], to_x[d])
-        to_sibling(plane, 1)
-        to_sibling(plane, 3)
-
-    def x_finish(plane):
-        for d in range(2):
-            i = plane * 2 + d
-            got(keys_ref.at[block(plane, 2), core, parts[d]], x2send.at[i], x2got.at[i])
-        to_sibling(plane, 2)
+    origin = (3, 1)
+
+    def own_first():
+        for d in range(2):
+            go(at(0, 0, parts[d]), x1send.at[d], x1got.at[d], to_x[d])
+
+    def own_second():
+        for d in range(2):
+            go(at(0, 0, parts[1 - d]), x1send.at[2 + d], x1got.at[2 + d], to_x[d])
+
+    def own_onward():
+        for d in range(2):
+            ref = at(0, origin[d], parts[d])
+            got(ref, x1send.at[d], x1got.at[d])
+            go(ref, x2send.at[d], x2got.at[d], to_x[d])
+
+    def own_near():
+        for d in range(2):
+            got(at(0, origin[d], parts[1 - d]), x1send.at[2 + d], x1got.at[2 + d])
+            to_sibling(0, origin[d])
+
+    def own_far():
+        for d in range(2):
+            got(at(0, 2, parts[d]), x2send.at[d], x2got.at[d])
+        to_sibling(0, 2)
+
+    def y_step1(r):
+        for d in range(2):
+            i = r * 2 + d
+            go(at(1, r, strip(y)), y1send.at[i], y1got.at[i], to_y[d])
 
     def from_z():
-        got(keys_ref.at[block(1, 0), core], zsend.at[0], zgot.at[0])
-        x_step1(1)
-        to_sibling(1, 0)
-
-    go(keys_ref.at[mine, core], zsend.at[0], zgot.at[0], to_z)
-    x_step1(0)
+        got(at(1, 0, strip(y)), zsend.at[0], zgot.at[0])
+        for d in range(2):
+            go(at(1, 0, strip(y)), s1send.at[d], s1got.at[d], to_x[d])
+        y_step1(0)
+
+    def strips_onward():
+        for d in range(2):
+            got(at(1, origin[d], strip(y)), s1send.at[d], s1got.at[d])
+            go(at(1, origin[d], strip_half(y, d)), s2send.at[d], s2got.at[d], to_x[d])
+        y_step1(1)
+        y_step1(3)
+
+    def strips_far():
+        for d in range(2):
+            got(at(1, 2, strip_half(y, d)), s2send.at[d], s2got.at[d])
+        y_step1(2)
+
+    def y_step2(r):
+        for d, source in enumerate((y_down, y_up)):
+            i = r * 2 + d
+            got(at(1, r, strip(source)), y1send.at[i], y1got.at[i])
+            go(at(1, r, strip_half(source, d)), y2send.at[i], y2got.at[i], to_y[d])
+
+    def y_finish(r):
+        for d in range(2):
+            i = r * 2 + d
+            got(at(1, r, strip_half(y_far, d)), y2send.at[i], y2got.at[i])
+        to_sibling(1, r)
+
+    def queries(start, stop):
+        for h in range(start, stop):
+            q = q_ref[h].astype(jnp.float32).T.astype(jnp.bfloat16)
+            lat = jnp.dot(q[:, :NOPE], uk_ref[h], preferred_element_type=jnp.float32)
+            qf_ref[h, :, :LAT] = lat.astype(jnp.bfloat16)
+            qf_ref[h, :, LAT:] = q[:, NOPE:]
+
+    go(at(0, 0, strip(y)), zsend.at[0], zgot.at[0], to_z)
+    own_first()
     to_sibling(0, 0)
-
     loads[2].wait()
     loads[5].wait()
-    for h in range(heads):
-        q = q_ref[h].astype(jnp.float32).T.astype(jnp.bfloat16)
-        lat = jnp.dot(q[:, :NOPE], uk_ref[h], preferred_element_type=jnp.float32)
-        qf_ref[h, :, :LAT] = lat.astype(jnp.bfloat16)
-        qf_ref[h, :, LAT:] = q[:, NOPE:]
+    queries(0, heads // 2)
+    from_z()
+    own_second()
+    queries(heads // 2, heads)
 
     loads[3].wait()
     t0 = ctx * rows
@@ -186,29 +241,37 @@
         lax.fori_loop(0, count, one, 0)
 
     scores(mine, core, True)
-    from_z()
-    x_step2(0)
+    strips_onward()
+    own_onward()
     from_sibling(0, 0)
     tiles(0, 0, 1, 1 - core)
+    y_step2(0)
+    strips_far()
+    own_near()
+    y_step2(1)
+    y_step2(3)
     tiles(0, 1, 2, core)
-    x_step2(1)
-    x_finish(0)
+    y_finish(0)
+    own_far()
+    y_step2(2)
     tiles(1, 0, 1, core)
-    for r in (1, 3):
-        from_sibling(0, r)
+    from_sibling(0, 1)
+    from_sibling(0, 3)
+    y_finish(1)
+    y_finish(3)
+    tiles(0, 1, 2, 1 - core)
+    tiles(0, 2, 1, core)
+    y_finish(2)
     from_sibling(1, 0)
-    tiles(0, 1, 2, 1 - core)
     tiles(1, 0, 1, 1 - core)
-    x_finish(1)
     tiles(1, 1, 2, core)
-    tiles(0, 2, 1, core)
-    for r in (1, 3):
-        from_sibling(1, r)
+    from_sibling(0, 2)
+    tiles(0, 2, 1, 1 - core)
+    from_sibling(1, 1)
+    from_sibling(1, 3)
     tiles(1, 1, 2, 1 - core)
     tiles(1, 2, 1, core)
-    from_sibling(0, 2)
     from_sibling(1, 2)
-    tiles(0, 2, 1, 1 - core)
     tiles(1, 2, 1, 1 - core)
 
     @pl.when(core == 0)
@@ -287,7 +350,11 @@
             dma((6,)),
             dma((1,)), dma((1,)),
             dma((4,)), dma((4,)),
-            dma((4,)), dma((4,)),
+            dma((2,)), dma((2,)),
+            dma((2,)), dma((2,)),
+            dma((2,)), dma((2,)),
+            dma((8,)), dma((8,)),
+            dma((8,)), dma((8,)),
             dma((8,)), dma((8,)),
         ],
         compiler_params=pltpu.CompilerParams(
@@ -441,7 +508,7 @@
     return pl.pallas_call(
         reduce_kernel,
         out_shape=jax.ShapeDtypeStruct((rows, cols), jnp.bfloat16),
-        in_specs=[pl.BlockSpec(memory_space=pl.ANY)] * 2,
+        in_specs=[pl.BlockSpec(memory_space=pltpu.HBM)] * 2,
         out_specs=pl.BlockSpec(memory_space=pltpu.VMEM),
         scratch_shapes=[
             pltpu.VMEM((rows, inner), jnp.bfloat16),

time: 84.1 us -> 79.7 us (0.948)
  Pallas kernels: 81.5 us -> 77.7 us
    pallas_call x1, Pallas kernels: 52.5 us -> 50.1 us  [attend(): pl.pallas_call(attend_kernel, out_shape=jax.ShapeDtypeStruct((rows, heads...]
    pallas_call x1, Pallas kernels: 29 us -> 27.7 us  [project_and_reduce(): pl.pallas_call(reduce_kernel, out_shape=jax.ShapeDtypeStruct((rows, cols)...]
where the time goes in v5:
time: 79.7 us; the launch traced here: 79.6 us
  Pallas kernels  77.7 us (97%)
  local copies, waits for them, and re-layouts  1.8 us (2%)
    pallas_call x1, Pallas kernels, attend(): pl.pallas_call(attend_kernel, out_shape=jax.ShapeDtypeStruct((rows, heads...  50.1 us
    pallas_call x1, Pallas kernels, project_and_reduce(): pl.pallas_call(reduce_kernel, out_shape=jax.ShapeDtypeStruct((rows, cols)...  27.7 us
    unnamed x3, local copies, waits for them, and re-layouts  1.8 us

profile of v5, /device:TPU:70, one launch (start us, length us, event | category | flops | bytes accessed | tf_op | source)
XLA Modules:
  0.0 79.6 jit_solution(12505560759186893962)
XLA Ops:
  0.0 50.1 %attend.1.x_hbm = bf16[256,1024]{1,0:T(8,128)(2,1)} custom-call(s32[8]{0:T(128)} %lens_hbm.1, bf16[8,192,256]{2,1,0:T(8,128)(2,1)} %bitcast.3, bf16[576,256]{1,0:T(8,128)(2,1)} %bitcast.4, f32[1,256]{1,0:T(1,128)} %bitcast.5, bf16[8,128,512]{2,1,0:T(8,128)(2,1)} %uk_hbm.1, bf16[8,512,128]{2,1,0:T(8,128)(2,1)} %uv_hbm.1), custom_call_target="tpu_custom_call" | custom-call | tf_op jit(solution)/shard_map/attend/pallas_call | solution.py:331
  50.1 0.0 copy-start
  50.1 1.0 %copy-done = bf16[256,1024]{1,0:T(8,128)(2,1)S(1)} copy-done((bf16[256,1024]{1,0:T(8,128)(2,1)S(1)}, bf16[256,1024]{1,0:T(8,128)(2,1)}, u32[]{:S(2)}) %copy-start) | copy-done | bytes 524312
  51.1 27.7 %project_and_reduce.1 = bf16[256,896]{1,0:T(8,128)(2,1)S(1)} custom-call(bf16[256,1024]{1,0:T(8,128)(2,1)S(1)} %copy-done, bf16[1024,7168]{1,0:T(8,128)(2,1)} %w_ref.1), custom_call_target="tpu_custom_call" | custom-call | tf_op jit(solution)/shard_map/project_and_reduce/pallas_call | solution.py:508
  78.8 0.8 copy.9
Async XLA Ops:
  50.1 1.0 %copy-start = (bf16[256,1024]{1,0:T(8,128)(2,1)S(1)}, bf16[256,1024]{1,0:T(8,128)(2,1)}, u32[]{:S(2)}) copy-start(bf16[256,1024]{1,0:T(8,128)(2,1)} %attend.1.x_hbm) | copy-start | bytes 1572868

commit v6 on v5

--- a/solution.py
+++ b/solution.py
@@ -11,6 +11,7 @@
 VDIM = 128
 GROUP = 4
 NEG = -1e30
+TOO_FAR = 1 << 20
 MESH = pl.DeviceIdType.MESH
 EXP_SCALE = float(QDIM) ** -0.5 * 1.4426950408889634
 
@@ -20,7 +21,7 @@
     lens_ref, q_ref, latents_ref, scale_ref, uk_ref, uv_ref,
     keys_ref, qf_ref, s_ref, m_ref, l_ref, acc_ref, first_ref, load_sem,
     zsend, zgot, x1send, x1got, x2send, x2got, s1send, s1got, s2send, s2got,
-    y1send, y1got, y2send, y2got, csend, cgot,
+    y1send, y1got, y2send, y2got, csend, cgot, hsend, hgot,
 ):
     rows = latents_ref.shape[1]
     heads = q_ref.shape[0]
@@ -124,16 +125,30 @@
         for d in range(2):
             go(at(0, 0, parts[1 - d]), x1send.at[2 + d], x1got.at[2 + d], to_x[d])
 
+    def near(turn, d):
+        return at(0, origin[d], parts[d if turn == 0 else 1 - d])
+
+    def half_to_sibling(turn):
+        for d in range(2):
+            i = turn * 2 + d
+            go(near(turn, d), hsend.at[i], hgot.at[i], to_core)
+
+    def half_from_sibling(turn):
+        for d in range(2):
+            i = turn * 2 + d
+            ref = keys_ref.at[block(0, origin[d]), 1 - core, parts[d if turn == 0 else 1 - d]]
+            got(ref, hsend.at[i], hgot.at[i])
+
     def own_onward():
         for d in range(2):
-            ref = at(0, origin[d], parts[d])
-            got(ref, x1send.at[d], x1got.at[d])
-            go(ref, x2send.at[d], x2got.at[d], to_x[d])
+            got(near(0, d), x1send.at[d], x1got.at[d])
+            go(near(0, d), x2send.at[d], x2got.at[d], to_x[d])
+        half_to_sibling(0)
 
     def own_near():
         for d in range(2):
-            got(at(0, origin[d], parts[1 - d]), x1send.at[2 + d], x1got.at[2 + d])
-            to_sibling(0, origin[d])
+            got(near(1, d), x1send.at[2 + d], x1got.at[2 + d])
+        half_to_sibling(1)
 
     def own_far():
         for d in range(2):
@@ -175,8 +190,8 @@
             got(at(1, r, strip_half(y_far, d)), y2send.at[i], y2got.at[i])
         to_sibling(1, r)
 
-    def queries(start, stop):
-        for h in range(start, stop):
+    def queries():
+        for h in range(heads):
             q = q_ref[h].astype(jnp.float32).T.astype(jnp.bfloat16)
             lat = jnp.dot(q[:, :NOPE], uk_ref[h], preferred_element_type=jnp.float32)
             qf_ref[h, :, :LAT] = lat.astype(jnp.bfloat16)
@@ -187,10 +202,9 @@
     to_sibling(0, 0)
     loads[2].wait()
     loads[5].wait()
-    queries(0, heads // 2)
+    queries()
     from_z()
     own_second()
-    queries(heads // 2, heads)
 
     loads[3].wait()
     t0 = ctx * rows
@@ -203,30 +217,43 @@
     first_ref[...] = jnp.concatenate([first] * GROUP, axis=0)
     m_ref[...] = jnp.full_like(m_ref, NEG)
 
-    def scores(p, k, diagonal):
-        j = p * 2 + k
-        kpos = j * rows + lax.broadcasted_iota(jnp.int32, (1, 128), 1)
-
+    lane_iota = lax.broadcasted_iota(jnp.int32, (1, 128), 1)
+
+    def scores(pieces, whole, diagonal=False):
         def one_group(g, carry):
             q = qf_ref[pl.ds(g * GROUP, GROUP)].reshape(block_rows, -1)
+            if whole:
+                keys = keys_ref[pieces[0][0], pieces[0][1]]
+            else:
+                keys = jnp.concatenate([keys_ref[p, k, parts[part]] for p, k, part in pieces], axis=0)
             s = lax.dot_general(
-                q, keys_ref[p, k], (((1,), (1,)), ((), ())), preferred_element_type=jnp.float32
+                q, keys, (((1,), (1,)), ((), ())), preferred_element_type=jnp.float32
             )
             here = pl.ds(pl.multiple_of(g * block_rows, block_rows), block_rows)
             top = m_ref[here]
-            for lane in range(0, rows, 128):
-                allowed = first_ref[...] <= kpos + lane
+            for n, (p, k, part) in enumerate(pieces):
+                j = p * 2 + k
+                lane = part * (rows // 2)
+                base = jnp.where(j <= ctx, j * rows + lane, -TOO_FAR)
+                allowed = first_ref[...] <= base + lane_iota
                 if diagonal:
                     local = lax.broadcasted_iota(jnp.int32, (block_rows, 128), 0)
                     ahead = lane + lax.broadcasted_iota(jnp.int32, (block_rows, 128), 1)
                     allowed = allowed & (ahead <= lax.rem(local, rows))
-                part = jnp.where(allowed, s[:, lane : lane + 128], NEG)
-                s_ref[j, here, lane : lane + 128] = part
-                top = jnp.maximum(top, part)
+                one = jnp.where(allowed, s[:, n * 128 : (n + 1) * 128], NEG)
+                s_ref[j, here, lane : lane + 128] = one
+                top = jnp.maximum(top, one)
             m_ref[here] = top
             return carry
 
         lax.fori_loop(0, groups, one_group, 0)
+
+    def near_tile(turn, k):
+        below, above = block(0, origin[0]), block(0, origin[1])
+
+        @pl.when((below * 2 + k < ctx) | (above * 2 + k < ctx))
+        def _():
+            scores(((below, k, turn), (above, k, 1 - turn)), False)
 
     def tiles(plane, r, count, k):
         def one(i, carry):
@@ -234,36 +261,38 @@
 
             @pl.when(p * 2 + k < ctx)
             def _():
-                scores(p, k, False)
+                scores(((p, k, 0), (p, k, 1)), True)
 
             return carry
 
         lax.fori_loop(0, count, one, 0)
 
-    scores(mine, core, True)
+    scores(((mine, core, 0), (mine, core, 1)), True, True)
+    from_sibling(0, 0)
+    tiles(0, 0, 1, 1 - core)
     strips_onward()
     own_onward()
-    from_sibling(0, 0)
-    tiles(0, 0, 1, 1 - core)
+    near_tile(0, core)
     y_step2(0)
+    half_from_sibling(0)
+    near_tile(0, 1 - core)
+    own_near()
     strips_far()
-    own_near()
+    near_tile(1, core)
     y_step2(1)
     y_step2(3)
-    tiles(0, 1, 2, core)
     y_finish(0)
+    half_from_sibling(1)
+    near_tile(1, 1 - core)
     own_far()
     y_step2(2)
     tiles(1, 0, 1, core)
-    from_sibling(0, 1)
-    from_sibling(0, 3)
+    tiles(0, 2, 1, core)
     y_finish(1)
     y_finish(3)
-    tiles(0, 1, 2, 1 - core)
-    tiles(0, 2, 1, core)
-    y_finish(2)
     from_sibling(1, 0)
     tiles(1, 0, 1, 1 - core)
+    y_finish(2)
     tiles(1, 1, 2, core)
     from_sibling(0, 2)
     tiles(0, 2, 1, 1 - core)
@@ -356,6 +385,7 @@
             dma((8,)), dma((8,)),
             dma((8,)), dma((8,)),
             dma((8,)), dma((8,)),
+            dma((4,)), dma((4,)),
         ],
         compiler_params=pltpu.CompilerParams(
             collective_id=1, has_side_effects=True, vmem_limit_bytes=61 << 20
@@ -396,13 +426,12 @@
 
     load = pltpu.make_async_copy(x_hbm, x_ref, x_sem.at[0])
     load.start()
-    for k in range(8):
+    for k in range(2):
         fetch(k).start()
     barrier = pltpu.get_barrier_semaphore()
     for target in (up, down, across):
         pl.semaphore_signal(barrier, inc=1, device_id={"head": target}, device_id_type=MESH)
     load.wait()
-    pl.semaphore_wait(barrier, 3)
 
     pending = []
 
@@ -427,9 +456,13 @@
 
     def compute(k):
         fetch(k).wait()
+        if k + 2 < 8:
+            fetch(k + 2).start()
         own[k] = jnp.dot(x_ref[...], wbuf[k], preferred_element_type=jnp.float32).astype(
             jnp.bfloat16
         )
+        if k == 0:
+            pl.semaphore_wait(barrier, 3)
         shift, mine = blocks[k]
         if not mine:
             i = across_order.index(shift)
@@ -530,7 +563,7 @@
             dma((1,)), dma((1,)),
         ],
         compiler_params=pltpu.CompilerParams(
-            collective_id=0, has_side_effects=True, vmem_limit_bytes=40 << 20
+            collective_id=0, has_side_effects=True, vmem_limit_bytes=62 << 20
         ),
         name="project_and_reduce",
     )(head_out, w_o)

time: 79.7 us -> 78 us (0.979)
  Pallas kernels: 77.7 us -> 76 us
    pallas_call x1, Pallas kernels: 50.1 us -> 47.6 us  [attend(): pl.pallas_call(attend_kernel, out_shape=jax.ShapeDtypeStruct((rows, heads...]
    unnamed x3 -> x1, local copies, waits for them, and re-layouts: 1.8 us -> 1.82 us
where the time goes in v6:
time: 78 us; the launch traced here: 77.8 us
  Pallas kernels  76 us (97%)
  local copies, waits for them, and re-layouts  1.82 us (2%)
    pallas_call x1, Pallas kernels, attend(): pl.pallas_call(attend_kernel, out_shape=jax.ShapeDtypeStruct((rows, heads...  47.6 us
    pallas_call x1, Pallas kernels, project_and_reduce(): pl.pallas_call(reduce_kernel, out_shape=jax.ShapeDtypeStruct((rows, cols)...  28.4 us
    unnamed x1, local copies, waits for them, and re-layouts  1.82 us

profile of v6, /device:TPU:70, one launch (start us, length us, event | category | flops | bytes accessed | tf_op | source)
XLA Modules:
  0.0 77.8 jit_solution(5346396795950118791)
XLA Ops:
  0.0 47.6 %attend.1.x_hbm = bf16[256,1024]{1,0:T(8,128)(2,1)} custom-call(s32[8]{0:T(128)} %lens_hbm.1, bf16[8,192,256]{2,1,0:T(8,128)(2,1)} %bitcast.3, bf16[576,256]{1,0:T(8,128)(2,1)} %bitcast.4, f32[1,256]{1,0:T(1,128)} %bitcast.5, bf16[8,128,512]{2,1,0:T(8,128)(2,1)} %uk_hbm.1, bf16[8,512,128]{2,1,0:T(8,128)(2,1)} %uv_hbm.1), custom_call_target="tpu_custom_call" | custom-call | tf_op jit(solution)/shard_map/attend/pallas_call | solution.py:360
  47.6 28.4 %project_and_reduce.1 = bf16[256,896]{1,0:T(8,128)(2,1)} custom-call(bf16[256,1024]{1,0:T(8,128)(2,1)} %attend.1.x_hbm, bf16[1024,7168]{1,0:T(8,128)(2,1)} %w_ref.1), custom_call_target="tpu_custom_call" | custom-call | tf_op jit(solution)/shard_map/project_and_reduce/pallas_call | solution.py:541
  76.0 1.8 %copy.9 = bf16[256,896]{1,0:T(8,128)(2,1)} copy(bf16[256,896]{1,0:T(8,128)(2,1)} %project_and_reduce.1) | data formatting | bytes 917504

commit v7 on v6

--- a/solution.py
+++ b/solution.py
@@ -9,7 +9,7 @@
 NOPE = 128
 QDIM = 192
 VDIM = 128
-GROUP = 4
+GROUP = 8
 NEG = -1e30
 TOO_FAR = 1 << 20
 MESH = pl.DeviceIdType.MESH
@@ -496,14 +496,15 @@
     for k in range(6):
         compute(k)
     y_first_step2(0)
-    for k in range(6, 8):
-        compute(k)
-    y_first_step2(1)
+    compute(6)
 
     got(zrecv, 0, zsend, zgot, half)
     k = slot[(2, 1)]
     own[k, first] = add_rows(k, first, zrecv[0]).astype(jnp.bfloat16)
     step1(k, 0, ysecond1, s1send, s1got, 0)
+
+    compute(7)
+    y_first_step2(1)
 
     got(y2recv, 0, y2send, y2got, half)
     got(y2recv, 1, y2send, y2got, half)

time: 78 us -> 75.3 us (0.965)
  Pallas kernels: 76 us -> 73.3 us
    pallas_call x1, Pallas kernels: 47.6 us -> 44.4 us  [attend(): pl.pallas_call(attend_kernel, out_shape=jax.ShapeDtypeStruct((rows, heads...]
where the time goes in v7:
time: 75.3 us; the launch traced here: 75.1 us
  Pallas kernels  73.3 us (97%)
  local copies, waits for them, and re-layouts  1.82 us (2%)
    pallas_call x1, Pallas kernels, attend(): pl.pallas_call(attend_kernel, out_shape=jax.ShapeDtypeStruct((rows, heads...  44.4 us
    pallas_call x1, Pallas kernels, project_and_reduce(): pl.pallas_call(reduce_kernel, out_shape=jax.ShapeDtypeStruct((rows, cols)...  28.9 us
    unnamed x1, local copies, waits for them, and re-layouts  1.82 us

profile of v7, /device:TPU:70, one launch (start us, length us, event | category | flops | bytes accessed | tf_op | source)
XLA Modules:
  0.0 75.1 jit_solution(7524097912636602330)
XLA Ops:
  0.0 44.4 %attend.1.x_hbm = bf16[256,1024]{1,0:T(8,128)(2,1)} custom-call(s32[8]{0:T(128)} %lens_hbm.1, bf16[8,192,256]{2,1,0:T(8,128)(2,1)} %bitcast.3, bf16[576,256]{1,0:T(8,128)(2,1)} %bitcast.4, f32[1,256]{1,0:T(1,128)} %bitcast.5, bf16[8,128,512]{2,1,0:T(8,128)(2,1)} %uk_hbm.1, bf16[8,512,128]{2,1,0:T(8,128)(2,1)} %uv_hbm.1), custom_call_target="tpu_custom_call" | custom-call | tf_op jit(solution)/shard_map/attend/pallas_call | solution.py:360
  44.4 28.9 %project_and_reduce.1 = bf16[256,896]{1,0:T(8,128)(2,1)} custom-call(bf16[256,1024]{1,0:T(8,128)(2,1)} %attend.1.x_hbm, bf16[1024,7168]{1,0:T(8,128)(2,1)} %w_ref.1), custom_call_target="tpu_custom_call" | custom-call | tf_op jit(solution)/shard_map/project_and_reduce/pallas_call | solution.py:542
  73.3 1.8 %copy.9 = bf16[256,896]{1,0:T(8,128)(2,1)} copy(bf16[256,896]{1,0:T(8,128)(2,1)} %project_and_reduce.1) | data formatting | bytes 917504

commit v8 on v7

--- a/solution.py
+++ b/solution.py
@@ -303,9 +303,13 @@
     from_sibling(1, 2)
     tiles(1, 2, 1, 1 - core)
 
-    @pl.when(core == 0)
-    def _():
-        s_ref[ctx + 1] = jnp.full(s_ref.shape[1:], NEG, jnp.float32)
+    chunks = ctx // 4 + 1
+
+    def clear(j, carry):
+        s_ref[j] = jnp.full(s_ref.shape[1:], NEG, jnp.float32)
+        return carry
+
+    lax.fori_loop(ctx + 1, chunks * 4, clear, 0)
 
     loads[4].wait()
 
@@ -320,20 +324,20 @@
             top = m_ref[here]
             weights = []
             total = l_ref[...]
-            for k in range(2):
+            for k in range(4):
                 for lane in range(0, rows, 128):
-                    s = s_ref[2 * p + k, here, lane : lane + 128]
+                    s = s_ref[4 * p + k, here, lane : lane + 128]
                     w = jnp.exp2((s - top) * EXP_SCALE)
                     total = total + w
                     weights.append(w.astype(jnp.bfloat16))
             l_ref[...] = total
-            values = keys_ref[p, :, :, :LAT].reshape(2 * rows, LAT)
+            values = keys_ref[pl.ds(2 * p, 2), :, :, :LAT].reshape(4 * rows, LAT)
             acc_ref[...] += jnp.dot(
                 jnp.concatenate(weights, axis=1), values, preferred_element_type=jnp.float32
             )
             return carry
 
-        lax.fori_loop(0, ctx // 2 + 1, weigh, 0)
+        lax.fori_loop(0, chunks, weigh, 0)
         inverse = 1.0 / jnp.sum(l_ref[...], axis=1, keepdims=True)
         context = (acc_ref[...] * inverse).astype(jnp.bfloat16)
         for i in range(GROUP):

time: 75.3 us -> 74.8 us (level)
  Pallas kernels: 73.3 us -> 72.3 us
    pallas_call x1, Pallas kernels: 44.4 us -> 43.4 us  [attend(): pl.pallas_call(attend_kernel, out_shape=jax.ShapeDtypeStruct((rows, heads...]
where the time goes in v8:
time: 74.8 us; the launch traced here: 74.2 us
  Pallas kernels  72.3 us (97%)
  local copies, waits for them, and re-layouts  1.82 us (2%)
    pallas_call x1, Pallas kernels, attend(): pl.pallas_call(attend_kernel, out_shape=jax.ShapeDtypeStruct((rows, heads...  43.4 us
    pallas_call x1, Pallas kernels, project_and_reduce(): pl.pallas_call(reduce_kernel, out_shape=jax.ShapeDtypeStruct((rows, cols)...  28.9 us
    unnamed x1, local copies, waits for them, and re-layouts  1.82 us

profile of v8, /device:TPU:70, one launch (start us, length us, event | category | flops | bytes accessed | tf_op | source)
XLA Modules:
  0.0 74.2 jit_solution(12399706376173814326)
XLA Ops:
  0.0 43.4 %attend.1.x_hbm = bf16[256,1024]{1,0:T(8,128)(2,1)} custom-call(s32[8]{0:T(128)} %lens_hbm.1, bf16[8,192,256]{2,1,0:T(8,128)(2,1)} %bitcast.3, bf16[576,256]{1,0:T(8,128)(2,1)} %bitcast.4, f32[1,256]{1,0:T(1,128)} %bitcast.5, bf16[8,128,512]{2,1,0:T(8,128)(2,1)} %uk_hbm.1, bf16[8,512,128]{2,1,0:T(8,128)(2,1)} %uv_hbm.1), custom_call_target="tpu_custom_call" | custom-call | tf_op jit(solution)/shard_map/attend/pallas_call | solution.py:364
  43.4 28.9 %project_and_reduce.1 = bf16[256,896]{1,0:T(8,128)(2,1)} custom-call(bf16[256,1024]{1,0:T(8,128)(2,1)} %attend.1.x_hbm, bf16[1024,7168]{1,0:T(8,128)(2,1)} %w_ref.1), custom_call_target="tpu_custom_call" | custom-call | tf_op jit(solution)/shard_map/project_and_reduce/pallas_call | solution.py:546
  72.3 1.8 %copy.9 = bf16[256,896]{1,0:T(8,128)(2,1)} copy(bf16[256,896]{1,0:T(8,128)(2,1)} %project_and_reduce.1) | data formatting | bytes 917504

commit v9 on v8

--- a/solution.py
+++ b/solution.py
@@ -403,8 +403,12 @@
     wsem, zsend, zgot, y1send, y1got, y2send, y2got, s1send, s1got, s2send, s2got, lsend, lgot,
 ):
     cols = out_ref.shape[1]
-    half = out_ref.shape[0] // 2
-    quarter = half // 2
+    rows = out_ref.shape[0]
+    early = rows * 7 // 16
+    late = rows - early
+    down_rows = rows // 4
+    early_up = early - down_rows
+    late_up = late - down_rows
     me = lax.axis_index("head")
     y = lax.rem(me, 4)
     z = me // 4
@@ -413,8 +417,8 @@
     across = (1 - z) * 4 + y
     blocks = ((2, 0), (2, 1), (1, 0), (3, 0), (1, 1), (3, 1), (0, 0), (0, 1))
     slot = {key: k for k, key in enumerate(blocks)}
-    first = pl.ds(0, half)
-    second = pl.ds(half, half)
+    first = pl.ds(0, early)
+    second = pl.ds(early, late)
 
     def fetch(k):
         shift, mine = blocks[k]
@@ -446,14 +450,13 @@
     def across_copy(i, k):
         return send(own.at[k, first], zrecv.at[i], zsend.at[i], zgot.at[i], across)
 
-    def step1(k, base, buf, ssem, rsem, i):
-        go(send(own.at[k, pl.ds(base, quarter)], buf.at[i], ssem.at[i], rsem.at[i], up))
-        go(
-            send(
-                own.at[k, pl.ds(base + quarter, quarter)],
-                buf.at[i + 1], ssem.at[i + 1], rsem.at[i + 1], down,
-            )
-        )
+    def step1(k, base, upper, buf, ssem, rsem, i):
+        for n, target, start, count in (
+            (i, up, base, upper),
+            (i + 1, down, base + upper, down_rows),
+        ):
+            part = own.at[k, pl.ds(start, count)]
+            go(send(part, buf.at[n, pl.ds(0, count)], ssem.at[n], rsem.at[n], target))
 
     across_order = (2, 1, 3, 0)
     across_copies = {}
@@ -473,7 +476,7 @@
             across_copies[i] = across_copy(i, k)
             go(across_copies[i])
         if shift == 2:
-            step1(k, half, y1recv, y1send, y1got, 2 * mine)
+            step1(k, early, late_up, y1recv, y1send, y1got, 2 * mine)
 
     def add_rows(k, rows, *terms):
         total = own[k, rows].astype(jnp.float32)
@@ -483,56 +486,60 @@
 
     copies = {}
 
+    def got(buf, i, ssem, rsem, count):
+        send(
+            own.at[0, pl.ds(0, count)], buf.at[i, pl.ds(0, count)], ssem.at[i], rsem.at[i], across
+        ).wait_recv()
+
     def y_first_step2(mine):
-        for side, (shift, target, offset) in enumerate(((1, up, 0), (3, down, quarter))):
+        for side, (shift, target, offset, count) in enumerate(
+            ((1, up, early, late_up), (3, down, early + late_up, down_rows))
+        ):
             k = slot[(shift, mine)]
             i = 2 * mine + side
-            rows = pl.ds(half + offset, quarter)
-            send(
-                own.at[0, pl.ds(0, quarter)], y1recv.at[i], y1send.at[i], y1got.at[i], target
-            ).wait_recv()
-            own[k, rows] = add_rows(k, rows, y1recv[i]).astype(jnp.bfloat16)
+            part = pl.ds(offset, count)
+            got(y1recv, i, y1send, y1got, count)
+            own[k, part] = add_rows(k, part, y1recv[i, :count]).astype(jnp.bfloat16)
             go(send(own.at[k, second], y2recv.at[i], y2send.at[i], y2got.at[i], target))
-
-    def got(buf, i, ssem, rsem, rows):
-        send(own.at[0, pl.ds(0, rows)], buf.at[i], ssem.at[i], rsem.at[i], across).wait_recv()
 
     for k in range(6):
         compute(k)
     y_first_step2(0)
     compute(6)
 
-    got(zrecv, 0, zsend, zgot, half)
+    got(zrecv, 0, zsend, zgot, early)
     k = slot[(2, 1)]
     own[k, first] = add_rows(k, first, zrecv[0]).astype(jnp.bfloat16)
-    step1(k, 0, ysecond1, s1send, s1got, 0)
+    step1(k, 0, early_up, ysecond1, s1send, s1got, 0)
 
     compute(7)
     y_first_step2(1)
 
-    got(y2recv, 0, y2send, y2got, half)
-    got(y2recv, 1, y2send, y2got, half)
+    got(y2recv, 0, y2send, y2got, late)
+    got(y2recv, 1, y2send, y2got, late)
     k = slot[(0, 0)]
     own[k, second] = add_rows(k, second, y2recv[0], y2recv[1]).astype(jnp.bfloat16)
     go(send(own.at[k, second], zlast.at[0], lsend.at[0], lgot.at[0], across))
 
-    for side, (shift, target, offset) in enumerate(((1, up, 0), (3, down, quarter))):
+    for side, (shift, target, offset, count) in enumerate(
+        ((1, up, 0, early_up), (3, down, early_up, down_rows))
+    ):
         k = slot[(shift, 1)]
-        got(zrecv, 1 + side, zsend, zgot, half)
-        got(ysecond1, side, s1send, s1got, quarter)
+        got(zrecv, 1 + side, zsend, zgot, early)
+        got(ysecond1, side, s1send, s1got, count)
         own[k, first] = add_rows(k, first, zrecv[1 + side]).astype(jnp.bfloat16)
-        rows = pl.ds(offset, quarter)
-        own[k, rows] = add_rows(k, rows, ysecond1[side]).astype(jnp.bfloat16)
+        part = pl.ds(offset, count)
+        own[k, part] = add_rows(k, part, ysecond1[side, :count]).astype(jnp.bfloat16)
         go(send(own.at[k, first], ysecond2.at[side], s2send.at[side], s2got.at[side], target))
 
     k = slot[(0, 1)]
-    got(y2recv, 2, y2send, y2got, half)
-    got(y2recv, 3, y2send, y2got, half)
-    got(zlast, 0, lsend, lgot, half)
+    got(y2recv, 2, y2send, y2got, late)
+    got(y2recv, 3, y2send, y2got, late)
+    got(zlast, 0, lsend, lgot, late)
     out_ref[second] = add_rows(k, second, y2recv[2], y2recv[3], zlast[0]).astype(jnp.bfloat16)
-    got(zrecv, 3, zsend, zgot, half)
-    got(ysecond2, 0, s2send, s2got, half)
-    got(ysecond2, 1, s2send, s2got, half)
+    got(zrecv, 3, zsend, zgot, early)
+    got(ysecond2, 0, s2send, s2got, early)
+    got(ysecond2, 1, s2send, s2got, early)
     out_ref[first] = add_rows(k, first, zrecv[3], ysecond2[0], ysecond2[1]).astype(jnp.bfloat16)
     for copy in pending:
         copy.wait_send()
@@ -541,7 +548,9 @@
 def project_and_reduce(head_out, w_o):
     rows, inner = head_out.shape
     cols = w_o.shape[1] // 8
-    half = rows // 2
+    early = rows * 7 // 16
+    late = rows - early
+    late_up = late - rows // 4
     dma = pltpu.SemaphoreType.DMA
     return pl.pallas_call(
         reduce_kernel,
@@ -553,12 +562,12 @@
             dma((1,)),
             pltpu.VMEM((8, inner, cols), jnp.bfloat16),
             pltpu.VMEM((8, rows, cols), jnp.bfloat16),
-            pltpu.VMEM((4, half, cols), jnp.bfloat16),
-            pltpu.VMEM((4, half // 2, cols), jnp.bfloat16),
-            pltpu.VMEM((4, half, cols), jnp.bfloat16),
-            pltpu.VMEM((2, half // 2, cols), jnp.bfloat16),
-            pltpu.VMEM((2, half, cols), jnp.bfloat16),
-            pltpu.VMEM((1, half, cols), jnp.bfloat16),
+            pltpu.VMEM((4, early, cols), jnp.bfloat16),
+            pltpu.VMEM((4, late_up, cols), jnp.bfloat16),
+            pltpu.VMEM((4, late, cols), jnp.bfloat16),
+            pltpu.VMEM((2, rows // 4, cols), jnp.bfloat16),
+            pltpu.VMEM((2, early, cols), jnp.bfloat16),
+            pltpu.VMEM((1, late, cols), jnp.bfloat16),
             dma((8,)),
             dma((4,)), dma((4,)),
             dma((4,)), dma((4,)),

time: 74.8 us -> 73.4 us (0.981)
  Pallas kernels: 72.3 us -> 71.1 us
    pallas_call x1, Pallas kernels: 28.9 us -> 27.7 us  [project_and_reduce(): pl.pallas_call(reduce_kernel, out_shape=jax.ShapeDtypeStruct((rows, cols)...]
where the time goes in v9:
time: 73.4 us; the launch traced here: 73 us
  Pallas kernels  71.1 us (97%)
  local copies, waits for them, and re-layouts  1.82 us (2%)
    pallas_call x1, Pallas kernels, attend(): pl.pallas_call(attend_kernel, out_shape=jax.ShapeDtypeStruct((rows, heads...  43.4 us
    pallas_call x1, Pallas kernels, project_and_reduce(): pl.pallas_call(reduce_kernel, out_shape=jax.ShapeDtypeStruct((rows, cols)...  27.7 us
    unnamed x1, local copies, waits for them, and re-layouts  1.82 us

profile of v9, /device:TPU:70, one launch (start us, length us, event | category | flops | bytes accessed | tf_op | source)
XLA Modules:
  0.0 73.0 jit_solution(15634306277695407039)
XLA Ops:
  0.0 43.4 %attend.1.x_hbm = bf16[256,1024]{1,0:T(8,128)(2,1)} custom-call(s32[8]{0:T(128)} %lens_hbm.1, bf16[8,192,256]{2,1,0:T(8,128)(2,1)} %bitcast.3, bf16[576,256]{1,0:T(8,128)(2,1)} %bitcast.4, f32[1,256]{1,0:T(1,128)} %bitcast.5, bf16[8,128,512]{2,1,0:T(8,128)(2,1)} %uk_hbm.1, bf16[8,512,128]{2,1,0:T(8,128)(2,1)} %uv_hbm.1), custom_call_target="tpu_custom_call" | custom-call | tf_op jit(solution)/shard_map/attend/pallas_call | solution.py:364
  43.4 27.7 %project_and_reduce.1 = bf16[256,896]{1,0:T(8,128)(2,1)} custom-call(bf16[256,1024]{1,0:T(8,128)(2,1)} %attend.1.x_hbm, bf16[1024,7168]{1,0:T(8,128)(2,1)} %w_ref.1), custom_call_target="tpu_custom_call" | custom-call | tf_op jit(solution)/shard_map/project_and_reduce/pallas_call | solution.py:555
  71.1 1.8 %copy.9 = bf16[256,896]{1,0:T(8,128)(2,1)} copy(bf16[256,896]{1,0:T(8,128)(2,1)} %project_and_reduce.1) | data formatting | bytes 917504
